TPU v7x, 512 devices: a whole 4x4x16 slice. The times are simulated.
512 devices in a mesh: blk: 64 (over z_lo, x, core), group: 8 (over z_hi, y).
Axes of the slice: x: 4, y: 4, z: 16 (z_hi: 2, z_lo: 8; z = z_hi * 8 + z_lo), core: 2. Of those that a mesh axis runs over, the one named last changes fastest.
Arguments:
- user_factors: float32 [8, 65536, 256], P('group', 'blk'), may hold values from -1.5 to 1.5
- item_factors: float32 [8, 16384, 256], P('group', 'blk'), may hold values from -1.5 to 1.5
- ratings: bfloat16 [8, 64, 8, 2, 256, 256], P('group', 'blk'), may hold values from -6 to 6
- tile_rows: int32 [8, 64, 8, 2], P('group', 'blk'), may hold values from 0 to 3, as said below
- counts: int32 [8, 64, 8], P('group', 'blk'), may hold values from 0 to 2
- plan: int32 [8, 64], replicated, may hold values from 0 to 63, as said below
Outputs:
- user_out: float32 [8, 65536, 256], P('group', 'blk')
- received: bfloat16 [8, 64, 4, 256, 256], P('group', 'blk')
Inputs may be any that keep to these rules, and one draw needn't show every extreme that they name: `tile_rows`: within one stop of one device the 2 entries differ. `plan`: in every group no device receives more than 4 blocks, and some device receives exactly 4.
All inputs are finite; a program needn't handle non-finite values.
Results may differ from a plain program's by a relative error of at most 0.006.
Values may be sent and summed in bfloat16 or wider, within the bound.
No kernel may reach another device: no remote copies, remote signals or barrier semaphores. Data moves between devices by JAX's collectives and lax.ppermute only.
A program may use at most 64 MiB of HBM per device.

v0:
```python
import functools

import jax
import jax.numpy as jnp
from jax import lax
from jax.experimental import pallas as pl
from jax.experimental.pallas import tpu as pltpu
from jax.sharding import PartitionSpec as P


CAP = 4
PLANE = 8
LAG = 2


FIRST_LIMIT = 62_500_000

learn_rate = 0.01
shrinkage = 0.05

VMEM = pl.BlockSpec(memory_space=pltpu.VMEM)
SMEM = pl.BlockSpec(memory_space=pltpu.SMEM)
ANY = pl.BlockSpec(memory_space=pl.ANY)
HBM = pl.BlockSpec(memory_space=pltpu.MemorySpace.HBM)
F32 = jnp.float32
BF16 = jnp.bfloat16


def call(
    body, out_shape, in_specs, out_specs, scratch=(), flops=0, moved=1 << 20, alias={},
    limit=12 << 20,
):
    return pl.pallas_call(
        body,
        out_shape=out_shape,
        in_specs=in_specs,
        out_specs=out_specs,
        scratch_shapes=scratch,
        input_output_aliases=alias,
        cost_estimate=pl.CostEstimate(flops=flops, bytes_accessed=moved, transcendentals=0),
        compiler_params=pltpu.CompilerParams(vmem_limit_bytes=limit),
    )


def stop_at(slot, inner, stops):
    if slot <= inner and slot < stops:
        return slot
    return slot - LAG if inner + LAG < slot < stops + LAG else None


def plan_slot(slot, stops, count_ref):
    inner = lax.rem(lax.axis_index("blk"), PLANE)
    early = jnp.logical_and(slot <= inner, slot < stops)
    late = jnp.logical_and(slot > inner + LAG, slot < stops + LAG)
    active = jnp.logical_or(early, late)
    stop = jnp.clip(jnp.where(late, slot - LAG, slot), 0, stops - 1)
    count = jnp.where(active, count_ref[stop], 0)
    crossed = jnp.logical_and(late, inner == 0)
    return active, stop, count, crossed


def fetch(stop, count, row_ref, user_ref, low_ref, rated_ref, tiles, copy):
    tile = tiles.shape[1]
    for c in range(tiles.shape[0]):
        rows = pl.ds(c * tile, tile)

        @pl.when(c < count)
        def _():
            first = pl.multiple_of(row_ref[c, stop] * tile, tile)
            low_ref[rows, :] = user_ref[pl.ds(first, tile), :].astype(BF16)

        @pl.when(c >= count)
        def _():
            low_ref[rows, :] = jnp.zeros((tile, low_ref.shape[1]), BF16)
            rated_ref[:, rows] = jnp.zeros((rated_ref.shape[0], tile), BF16)

    copy.wait()
    for c in range(tiles.shape[0]):
        rows = pl.ds(c * tile, tile)

        @pl.when(c < count)
        def _():
            rated_ref[:, rows] = tiles[c].T


def update_items(exact, item_low, count, low_ref, rated_ref, residual_ref, item_ref):
    item_ref[...] = item_low
    tile = item_ref.shape[0]
    grad = None
    for c in range(low_ref.shape[0] // tile):
        span = slice(c * tile, (c + 1) * tile)
        low = low_ref[span, :]
        predicted = lax.dot_general(
            item_low, low, (((1,), (1,)), ((), ())), preferred_element_type=F32
        )
        residual = (rated_ref[:, span].astype(F32) - predicted).astype(BF16)
        residual_ref[:, span] = residual
        part = jnp.dot(residual, low, preferred_element_type=F32)
        grad = part if grad is None else grad + part
    decay = shrinkage * count.astype(F32)
    return (exact + learn_rate * (grad - decay * exact)).astype(BF16)


def first_body(
    count_hbm, row_hbm, user_hbm, item_hbm, ratings_hbm, next_ref, residual_ref, item_ref,
    count_ref, row_ref, user_ref, exact_ref, tiles, low_ref, rated_ref, sems,
):
    pairs = [
        (count_hbm, count_ref),
        (row_hbm, row_ref),
        (user_hbm, user_ref),
        (item_hbm, exact_ref),
        (ratings_hbm.at[0], tiles),
    ]
    moves = [pltpu.make_async_copy(*pair, sems.at[n]) for n, pair in enumerate(pairs)]
    for move in moves:
        move.start()
    for move in moves[:3]:
        move.wait()
    count = count_ref[0]
    fetch(0, count, row_ref, user_ref, low_ref, rated_ref, tiles, moves[4])
    moves[3].wait()
    exact = exact_ref[...]
    next_ref[...] = update_items(
        exact, exact.astype(BF16), count, low_ref, rated_ref, residual_ref, item_ref
    )


def item_body(slot, stops, last, n_in, count_ref, *refs):
    sources = refs[:n_in]
    low_ref, rated_ref, next_ref, residual_ref, item_ref = refs[n_in:]
    active, _, count, crossed = plan_slot(slot, stops, count_ref)

    def emit(block):
        if last:
            groups, halves, rows, columns = next_ref.shape
            for h in range(halves):
                half = block[:, h * columns : (h + 1) * columns]
                next_ref[:, h] = half.reshape(groups, rows, columns)
        else:
            next_ref[...] = block

    @pl.when(active)
    def _():
        item_low = sources[0][...]
        if n_in == 3:
            item_low = jnp.where(crossed, sources[2][...], item_low)
        exact = item_low.astype(F32)
        emit(update_items(exact, item_low, count, low_ref, rated_ref, residual_ref, item_ref))

    @pl.when(jnp.logical_not(active))
    def _():
        emit(sources[1][...])


def user_body(slot, stops, last, count_ref, row_ref, residual_ref, item_ref, user_ref, *refs):
    _, stop, count, _ = plan_slot(slot, stops, count_ref)
    if last:
        (out_ref,) = refs
    else:
        ratings_ref, out_ref, low_ref, rated_ref, tiles, sem = refs
        next_active, next_stop, next_count, _ = plan_slot(slot + 1, stops, count_ref)
        copy = pltpu.make_async_copy(ratings_ref.at[next_stop], tiles, sem)
        pl.when(next_active)(copy.start)
    tile = item_ref.shape[0]
    out_ref[...] = user_ref[...]
    for c in range(residual_ref.shape[1] // tile):

        @pl.when(c < count)
        def _():
            step = lax.dot_general(
                residual_ref[:, c * tile : (c + 1) * tile],
                item_ref[...],
                (((0,), (0,)), ((), ())),
                preferred_element_type=F32,
            )
            rows = pl.ds(pl.multiple_of(row_ref[c, stop] * tile, tile), tile)
            before = user_ref[rows, :]
            out_ref[rows, :] = before + learn_rate * (step - shrinkage * before)

    if not last:

        @pl.when(next_active)
        def _():
            fetch(next_stop, next_count, row_ref, out_ref, low_ref, rated_ref, tiles, copy)


def route_body(stops, plan_ref, index_ref, filled):
    groups, blocks = plan_ref.shape
    group = lax.rem(lax.axis_index("group") + groups - 1, groups)

    @pl.loop(0, blocks)
    def _(d):
        filled[d] = 0
        for c in range(CAP):
            index_ref[d * CAP + c] = -1

    @pl.loop(0, blocks)
    def _(k):
        dest = plan_ref[group, k]
        place = filled[dest]
        filled[dest] = place + 1
        index_ref[dest * CAP + place] = lax.rem(k + (stops - 1), blocks)


def pick_body(index_ref, pieces_ref, out_ref):
    @pl.loop(0, out_ref.shape[0], unroll=8)
    def _(d):
        for c in range(CAP):
            at = index_ref[d * CAP + c]
            piece = pieces_ref[jnp.maximum(at, 0)]
            out_ref[d, c] = jnp.where(at >= 0, piece, jnp.zeros_like(piece))


def place_body(pieces_ref, out_ref):
    groups, halves, slots, rows, columns = pieces_ref.shape
    for c in range(slots):
        for h in range(halves):
            out_ref[c, :, h * columns : (h + 1) * columns] = pieces_ref[:, h, c].reshape(
                groups * rows, columns
            )


def shards(user_factors, item_factors, ratings, tile_rows, counts, plan):
    users = user_factors[0]
    rating_tiles = ratings[0, 0]
    row_table = tile_rows[0, 0].T
    count_table = counts[0, 0]
    stops, tiles_at_stop, tile, _ = rating_tiles.shape
    blocks = lax.axis_size("blk")
    groups = lax.axis_size("group")
    items, rank = item_factors.shape[1:]
    wide = tiles_at_stop * tile
    slots = stops + LAG

    index = call(
        functools.partial(route_body, stops),
        jax.ShapeDtypeStruct((blocks * CAP,), jnp.int32),
        [SMEM],
        SMEM,
        [pltpu.SMEM((blocks,), jnp.int32)],
        moved=4 * blocks,
    )(plan)

    low_shape = jax.ShapeDtypeStruct((wide, rank), BF16)
    rated_shape = jax.ShapeDtypeStruct((items, wide), BF16)
    block_shape = jax.ShapeDtypeStruct((items, rank), BF16)
    piece_shape = jax.ShapeDtypeStruct((items // 8, rank // 128, 8, 128), BF16)
    user_shape = jax.ShapeDtypeStruct(users.shape, F32)
    tile_scratch = [pltpu.VMEM((tiles_at_stop, tile, tile), BF16), pltpu.SemaphoreType.DMA]
    block, residual, item_low = call(
        first_body,
        (block_shape, rated_shape, block_shape),
        [HBM] * 5,
        (VMEM, VMEM, VMEM),
        [
            pltpu.SMEM(count_table.shape, jnp.int32),
            pltpu.SMEM(row_table.shape, jnp.int32),
            pltpu.VMEM(users.shape, F32),
            pltpu.VMEM((items, rank), F32),
            tile_scratch[0],
            pltpu.VMEM(low_shape.shape, BF16),
            pltpu.VMEM(rated_shape.shape, BF16),
            pltpu.SemaphoreType.DMA((5,)),
        ],
        4 * items * wide * rank,
        limit=FIRST_LIMIT,
    )(count_table, row_table, users, item_factors[0], rating_tiles)

    across = [(b, (b + 1) % blocks) for b in range(PLANE - 1, blocks, PLANE)]
    crossing = {}
    for slot in range(slots):
        last = slot == slots - 1
        if slot > 0:
            block, residual, item_low = call(
                functools.partial(item_body, slot, stops, last, len(arrived)),
                (piece_shape if last else block_shape, rated_shape, block_shape),
                [SMEM] + [VMEM] * (len(arrived) + 2),
                (VMEM, VMEM, VMEM),
                (),
                4 * items * wide * rank,
            )(count_table, *arrived, low, rated)
        if not last:
            within = [
                (b, b + 1)
                for b in range(blocks)
                if b % PLANE != PLANE - 1
                and stop_at(slot, b % PLANE, stops) is not None
                and stop_at(slot + 1, b % PLANE + 1, stops) == stop_at(slot, b % PLANE, stops) + 1
            ]
            arrived = [lax.ppermute(block, "blk", within), block]
            if slot < stops - 1:
                crossing[slot + 1 + LAG] = lax.ppermute(block, "blk", across)
            if slot + 1 in crossing:
                arrived.append(crossing[slot + 1])
        body = functools.partial(user_body, slot, stops, last)
        operands = (count_table, row_table, residual, item_low, users)
        flops = 2 * wide * items * rank
        if last:
            users = call(
                body, user_shape, [SMEM, SMEM, VMEM, VMEM, VMEM], VMEM, (), flops
            )(*operands)
        else:
            users, low, rated = call(
                body,
                (user_shape, low_shape, rated_shape),
                [SMEM, SMEM, VMEM, VMEM, VMEM, ANY],
                (VMEM, VMEM, VMEM),
                tile_scratch,
                flops,
                alias={4: 0} if slot else {},
            )(*operands, rating_tiles)

    pieces = block.reshape(blocks, -1, 128)
    shifted = lax.ppermute(pieces, "group", [(g, (g + 1) % groups) for g in range(groups)])
    spread = lax.all_to_all(shifted, "blk", split_axis=0, concat_axis=0, tiled=True)
    picked = call(
        pick_body, jax.ShapeDtypeStruct((blocks, CAP) + pieces.shape[1:], BF16), [SMEM, VMEM], VMEM
    )(index, spread)
    landed = lax.all_to_all(picked, "blk", split_axis=0, concat_axis=0, tiled=True)
    landed = landed.reshape(blocks, CAP, -1, 8, 128).transpose(0, 2, 1, 3, 4)
    received = call(
        place_body, jax.ShapeDtypeStruct((CAP, items, rank), BF16), [VMEM], VMEM
    )(landed.reshape(items // 8, rank // 128, CAP, 8, 128))
    return (users[None], received[None, None])


def solution(mesh):
    in_specs = (
        P("group", "blk", None),
        P("group", "blk", None),
        P("group", "blk", None, None, None, None),
        P("group", "blk", None, None),
        P("group", "blk", None),
        P(),
    )
    out_specs = (P("group", "blk", None), P("group", "blk", None, None, None))
    return jax.shard_map(shards, mesh=mesh, in_specs=in_specs, out_specs=out_specs, check_vma=False)
```

profile of v0, /device:TPU:1, one launch (start us, length us, event | category | flops | bytes accessed | tf_op | source)
XLA Modules:
  0.0 164.4 jit_solution(16733145221353848299)
XLA Ops:
  0.7 2.9 %shard_map.77 = (bf16[256,256]{1,0:T(8,128)(2,1)}, bf16[256,512]{1,0:T(8,128)(2,1)}, bf16[256,256]{1,0:T(8,128)(2,1)}) custom-call(s32[8]{0:T(128)} %bitcast.24, s32[2,8]{1,0:T(2,128)} %bitcast.44, f32[1024,256]{1,0:T(8,128)} %bitcast.21, f32[256,256]{1,0:T(8,128)} %bitcast.58, bf16[8,2,256,256]{3,2,1,0:T(8,128)(2,1)} %bitcast.11), custom_call_target="tpu_custom_call" | custom-call | flops 134217728 | bytes 1048576 | tf_op jit(solution)/shard_map/pallas_call | solution.py:251
  3.6 4.4 %collective-permute-start = (bf16[256,256]{1,0:T(8,128)(2,1)}, bf16[256,256]{1,0:T(8,128)(2,1)S(1)}, u32[]{:S(2)}, u32[]{:S(2)}) collective-permute-start(bf16[256,256]{1,0:T(8,128)(2,1)} %get-tuple-element.59.refs_1_), channel_id=1, source_target_pairs={{0,8},{8,16},{16,24},{24,32},{32,40},{40,48},{48,56},{64,72},{72,8... | collective-permute-start | bytes 393224 | tf_op jit(solution)/shard_map/ppermute | solution.py:291
  11.1 1.5 collective-permute-done.refs_0_
  13.7 1.8 %collective-permute-start.1 = (bf16[256,256]{1,0:T(8,128)(2,1)S(1)}, bf16[256,256]{1,0:T(8,128)(2,1)S(1)}, u32[]{:S(2)}, u32[]{:S(2)}) collective-permute-start(bf16[256,256]{1,0:T(8,128)(2,1)S(1)} %get-tuple-element.64.refs_1_), channel_id=1, source_target_pairs={{8,16},{16,24},{24,32},{32,40},{40,48},{48,56},{72,80},{80,88},{88... | collective-permute-start | bytes 393224 | tf_op jit(solution)/shard_map/ppermute | solution.py:291
  23.7 10.2 %collective-permute-done.4.refs_0_ = bf16[256,256]{1,0:T(8,128)(2,1)S(1)} collective-permute-done((bf16[256,256]{1,0:T(8,128)(2,1)S(1)}, bf16[256,256]{1,0:T(8,128)(2,1)S(1)}, u32[]{:S(2)}, u32[]{:S(2)}) %collective-permute-start.4) | collective-permute-done | bytes 131104 | tf_op jit(solution)/shard_map/ppermute | solution.py:291
  35.0 1.9 %collective-permute-start.6 = (bf16[256,256]{1,0:T(8,128)(2,1)S(1)}, bf16[256,256]{1,0:T(8,128)(2,1)S(1)}, u32[]{:S(2)}, u32[]{:S(2)}) collective-permute-start(bf16[256,256]{1,0:T(8,128)(2,1)S(1)} %get-tuple-element.82.refs_1_), channel_id=1, source_target_pairs={{0,8},{8,16},{32,40},{40,48},{48,56},{64,72},{72,80},{96,104},{104... | collective-permute-start | bytes 393224 | tf_op jit(solution)/shard_map/ppermute | solution.py:291
  37.6 1.4 shard_map.86
  40.1 4.1 %collective-permute-start.8 = (bf16[256,256]{1,0:T(8,128)(2,1)S(1)}, bf16[256,256]{1,0:T(8,128)(2,1)S(1)}, u32[]{:S(2)}, u32[]{:S(2)}) collective-permute-start(bf16[256,256]{1,0:T(8,128)(2,1)S(1)} %get-tuple-element.88.refs_1_), channel_id=1, source_target_pairs={{0,8},{8,16},{16,24},{40,48},{48,56},{64,72},{72,80},{80,88},{104,... | collective-permute-start | bytes 393224 | tf_op jit(solution)/shard_map/ppermute | solution.py:291
  44.9 1.4 shard_map.88
  46.4 4.9 %collective-permute-done.8.refs_0_ = bf16[256,256]{1,0:T(8,128)(2,1)S(1)} collective-permute-done((bf16[256,256]{1,0:T(8,128)(2,1)S(1)}, bf16[256,256]{1,0:T(8,128)(2,1)S(1)}, u32[]{:S(2)}, u32[]{:S(2)}) %collective-permute-start.8) | collective-permute-done | bytes 131104 | tf_op jit(solution)/shard_map/ppermute | solution.py:291
  52.3 1.9 %collective-permute-start.10 = (bf16[256,256]{1,0:T(8,128)(2,1)S(1)}, bf16[256,256]{1,0:T(8,128)(2,1)S(1)}, u32[]{:S(2)}, u32[]{:S(2)}) collective-permute-start(bf16[256,256]{1,0:T(8,128)(2,1)S(1)} %get-tuple-element.94.refs_1_), channel_id=1, source_target_pairs={{0,8},{8,16},{16,24},{24,32},{48,56},{64,72},{72,80},{80,88},{88,9... | collective-permute-start | bytes 393224 | tf_op jit(solution)/shard_map/ppermute | solution.py:291
  55.0 1.4 shard_map.90
  57.5 4.1 %collective-permute-start.12 = (bf16[256,256]{1,0:T(8,128)(2,1)S(1)}, bf16[256,256]{1,0:T(8,128)(2,1)S(1)}, u32[]{:S(2)}, u32[]{:S(2)}) collective-permute-start(bf16[256,256]{1,0:T(8,128)(2,1)S(1)} %get-tuple-element.100.refs_1_), channel_id=1, source_target_pairs={{0,8},{8,16},{16,24},{24,32},{32,40},{64,72},{72,80},{80,88},{88,9... | collective-permute-start | bytes 393224 | tf_op jit(solution)/shard_map/ppermute | solution.py:291
  63.7 5.0 %collective-permute-done.12.refs_0_ = bf16[256,256]{1,0:T(8,128)(2,1)S(1)} collective-permute-done((bf16[256,256]{1,0:T(8,128)(2,1)S(1)}, bf16[256,256]{1,0:T(8,128)(2,1)S(1)}, u32[]{:S(2)}, u32[]{:S(2)}) %collective-permute-start.12) | collective-permute-done | bytes 131104 | tf_op jit(solution)/shard_map/ppermute | solution.py:291
  69.7 1.9 %collective-permute-start.14 = (bf16[256,256]{1,0:T(8,128)(2,1)S(1)}, bf16[256,256]{1,0:T(8,128)(2,1)S(1)}, u32[]{:S(2)}, u32[]{:S(2)}) collective-permute-start(bf16[256,256]{1,0:T(8,128)(2,1)S(1)} %get-tuple-element.106.refs_1_), channel_id=1, source_target_pairs={{0,8},{8,16},{16,24},{24,32},{32,40},{40,48},{64,72},{72,80},{80,8... | collective-permute-start | bytes 393224 | tf_op jit(solution)/shard_map/ppermute | solution.py:291
  74.9 2.5 %collective-permute-start.16 = (bf16[64,8,128]{2,1,0:T(8,128)(2,1)S(1)}, bf16[64,8,128]{2,1,0:T(8,128)(2,1)}, u32[]{:S(2)}, u32[]{:S(2)}) collective-permute-start(bf16[64,8,128]{2,1,0:T(8,128)(2,1)S(1)} %bitcast.55), channel_id=1, source_target_pairs={{0,1},{1,2},{2,3},{3,4},{4,5},{5,6},{6,7},{7,0},{8,9},{9,10},{10,1... | collective-permute-start | bytes 393224 | tf_op jit(solution)/shard_map/ppermute | solution.py:315
  77.4 18.9 %collective-permute-done.16 = bf16[64,8,128]{2,1,0:T(8,128)(2,1)} collective-permute-done((bf16[64,8,128]{2,1,0:T(8,128)(2,1)S(1)}, bf16[64,8,128]{2,1,0:T(8,128)(2,1)}, u32[]{:S(2)}, u32[]{:S(2)}) %collective-permute-start.16) | collective-permute-done | bytes 131104 | tf_op jit(solution)/shard_map/ppermute | solution.py:315
  96.3 14.6 %all-to-all-start = ((bf16[64,8,128]{2,1,0:T(8,128)(2,1)}), bf16[64,8,128]{2,1,0:T(8,128)(2,1)S(1)}, u32[]{:S(2)}, u32[]{:S(2)}) async-start(bf16[64,8,128]{2,1,0:T(8,128)(2,1)} %collective-permute-done.16), calls=%async_computation | async-start | bytes 262144 | tf_op jit(solution)/shard_map/all_to_all | solution.py:316
  110.9 2.4 %shard_map.97.index_ref = s32[256]{0:T(256)S(1)} custom-call(s32[8,64]{1,0:T(8,128)S(1)} %copy-done.7), custom_call_target="tpu_custom_call" | custom-call | bytes 256 | tf_op jit(solution)/shard_map/pallas_call | solution.py:236
  113.3 12.3 %all-to-all-done.pieces_ref = bf16[64,8,128]{2,1,0:T(8,128)(2,1)S(1)} async-done(((bf16[64,8,128]{2,1,0:T(8,128)(2,1)}), bf16[64,8,128]{2,1,0:T(8,128)(2,1)S(1)}, u32[]{:S(2)}, u32[]{:S(2)}) %all-to-all-start) | async-done | bytes 131104 | tf_op jit(solution)/shard_map/all_to_all | solution.py:316
  125.6 2.0 %shard_map.98 = bf16[64,4,8,128]{3,2,1,0:T(8,128)(2,1)} custom-call(s32[256]{0:T(256)S(1)} %shard_map.97.index_ref, bf16[64,8,128]{2,1,0:T(8,128)(2,1)S(1)} %all-to-all-done.pieces_ref), custom_call_target="tpu_custom_call" | custom-call | bytes 1048576 | tf_op jit(solution)/shard_map/pallas_call | solution.py:317
  127.6 5.7 %all-to-all-start.1 = ((bf16[64,4,8,128]{3,2,1,0:T(8,128)(2,1)}), bf16[64,4,8,128]{3,2,1,0:T(8,128)(2,1)S(1)}, u32[]{:S(2)}, u32[]{:S(2)}) async-start(bf16[64,4,8,128]{3,2,1,0:T(8,128)(2,1)} %shard_map.98), calls=%async_computation.1 | async-start | bytes 1048576 | tf_op jit(solution)/shard_map/all_to_all | solution.py:320
  133.4 1.8 %shard_map.96 = f32[1024,256]{1,0:T(8,128)} custom-call(s32[8]{0:T(128)S(1)} %bitcast.43, s32[2,8]{1,0:T(2,128)S(1)} %bitcast.54, bf16[256,512]{1,0:T(8,128)(2,1)S(1)} %get-tuple-element.112.residual_ref, bf16[256,256]{1,0:T(8,128)(2,1)S(1)} %get-tuple-element.113.item_ref, f32[1024,256]{1,0:T(8,128)S(1)} %get-tuple-element.114.user_ref), custom_call_target="tpu_custom_call" | custom-call | flops 67108864 | bytes 1048576 | tf_op jit(solution)/shard_map/pallas_call | solution.py:300
  135.2 28.3 %all-to-all-done.1 = bf16[64,4,8,128]{3,2,1,0:T(8,128)(2,1)S(1)} async-done(((bf16[64,4,8,128]{3,2,1,0:T(8,128)(2,1)}), bf16[64,4,8,128]{3,2,1,0:T(8,128)(2,1)S(1)}, u32[]{:S(2)}, u32[]{:S(2)}) %all-to-all-start.1) | async-done | bytes 524320 | tf_op jit(solution)/shard_map/all_to_all | solution.py:320
  (53 shorter events, 25.7 us)
Async XLA Ops:
  0.6 7.4 %copy-start.3 = (s32[1,1,8]{2,1,0:T(1,128)S(1)}, s32[1,1,8]{2,1,0:T(1,128)}, u32[]{:S(2)}) copy-start(s32[1,1,8]{2,1,0:T(1,128)} %param.10) | copy-start | bytes 100
  0.6 7.4 %copy-start.6 = (s32[1,1,8,2]{2,3,1,0:T(2,128)S(1)}, s32[1,1,8,2]{2,3,1,0:T(2,128)}, u32[]{:S(2)}) copy-start(s32[1,1,8,2]{2,3,1,0:T(2,128)} %param.9) | copy-start | bytes 196
  0.7 7.4 %copy-start = (bf16[1,1,8,2,256,256]{5,4,3,2,1,0:T(8,128)(2,1)S(1)}, bf16[1,1,8,2,256,256]{5,4,3,2,1,0:T(8,128)(2,1)}, u32[]{:S(2)}) copy-start(bf16[1,1,8,2,256,256]{5,4,3,2,1,0:T(8,128)(2,1)} %param.8) | copy-start | bytes 6291460
  0.7 7.4 %copy-start.1 = (f32[1,1024,256]{2,1,0:T(8,128)S(1)}, f32[1,1024,256]{2,1,0:T(8,128)}, u32[]{:S(2)}) copy-start(f32[1,1024,256]{2,1,0:T(8,128)} %param.6) | copy-start | bytes 3145732
  3.6 9.1 %collective-permute-start = (bf16[256,256]{1,0:T(8,128)(2,1)}, bf16[256,256]{1,0:T(8,128)(2,1)S(1)}, u32[]{:S(2)}, u32[]{:S(2)}) collective-permute-start(bf16[256,256]{1,0:T(8,128)(2,1)} %get-tuple-element.59.refs_1_), channel_id=1, source_target_pairs={{0,8},{8,16},{16,24},{24,32},{32,40},{40,48},{48,56},{64,72},{72,8... | collective-permute-start | bytes 393224 | tf_op jit(solution)/shard_map/ppermute | solution.py:291
  13.7 3.8 %collective-permute-start.1 = (bf16[256,256]{1,0:T(8,128)(2,1)S(1)}, bf16[256,256]{1,0:T(8,128)(2,1)S(1)}, u32[]{:S(2)}, u32[]{:S(2)}) collective-permute-start(bf16[256,256]{1,0:T(8,128)(2,1)S(1)} %get-tuple-element.64.refs_1_), channel_id=1, source_target_pairs={{8,16},{16,24},{24,32},{32,40},{40,48},{48,56},{72,80},{80,88},{88... | collective-permute-start | bytes 393224 | tf_op jit(solution)/shard_map/ppermute | solution.py:291
  15.6 4.6 %collective-permute-start.3 = (bf16[256,256]{1,0:T(8,128)(2,1)S(1)}, bf16[256,256]{1,0:T(8,128)(2,1)S(1)}, u32[]{:S(2)}, u32[]{:S(2)}) collective-permute-start(bf16[256,256]{1,0:T(8,128)(2,1)S(1)} %copy-done.5), channel_id=1, source_target_pairs={{56,64},{120,128},{184,192},{248,256},{312,320},{376,384},{440,448... | collective-permute-start | bytes 393224 | tf_op jit(solution)/shard_map/ppermute | solution.py:293
  18.1 2.1 %collective-permute-start.2 = (bf16[256,256]{1,0:T(8,128)(2,1)S(1)}, bf16[256,256]{1,0:T(8,128)(2,1)S(1)}, u32[]{:S(2)}, u32[]{:S(2)}) collective-permute-start(bf16[256,256]{1,0:T(8,128)(2,1)S(1)} %get-tuple-element.70.refs_1_), channel_id=1, source_target_pairs={{16,24},{24,32},{32,40},{40,48},{48,56},{80,88},{88,96},{96,104},{... | collective-permute-start | bytes 393224 | tf_op jit(solution)/shard_map/ppermute | solution.py:291
  18.7 5.0 %collective-permute-start.5 = (bf16[256,256]{1,0:T(8,128)(2,1)S(1)}, bf16[256,256]{1,0:T(8,128)(2,1)S(1)}, u32[]{:S(2)}, u32[]{:S(2)}) collective-permute-start(bf16[256,256]{1,0:T(8,128)(2,1)S(1)} %get-tuple-element.64.refs_1_), channel_id=1, source_target_pairs={{56,64},{120,128},{184,192},{248,256},{312,320},{376,384},{440,448... | collective-permute-start | bytes 393224 | tf_op jit(solution)/shard_map/ppermute | solution.py:293
  20.8 13.1 %collective-permute-start.4 = (bf16[256,256]{1,0:T(8,128)(2,1)S(1)}, bf16[256,256]{1,0:T(8,128)(2,1)S(1)}, u32[]{:S(2)}, u32[]{:S(2)}) collective-permute-start(bf16[256,256]{1,0:T(8,128)(2,1)S(1)} %get-tuple-element.76.refs_1_), channel_id=1, source_target_pairs={{0,8},{24,32},{32,40},{40,48},{48,56},{64,72},{88,96},{96,104},{10... | collective-permute-start | bytes 393224 | tf_op jit(solution)/shard_map/ppermute | solution.py:291
  22.1 17.0 %collective-permute-start.7 = (bf16[256,256]{1,0:T(8,128)(2,1)S(1)}, bf16[256,256]{1,0:T(8,128)(2,1)S(1)}, u32[]{:S(2)}, u32[]{:S(2)}) collective-permute-start(bf16[256,256]{1,0:T(8,128)(2,1)S(1)} %get-tuple-element.70.refs_1_), channel_id=1, source_target_pairs={{56,64},{120,128},{184,192},{248,256},{312,320},{376,384},{440,448... | collective-permute-start | bytes 393224 | tf_op jit(solution)/shard_map/ppermute | solution.py:293
  35.0 4.1 %collective-permute-start.6 = (bf16[256,256]{1,0:T(8,128)(2,1)S(1)}, bf16[256,256]{1,0:T(8,128)(2,1)S(1)}, u32[]{:S(2)}, u32[]{:S(2)}) collective-permute-start(bf16[256,256]{1,0:T(8,128)(2,1)S(1)} %get-tuple-element.82.refs_1_), channel_id=1, source_target_pairs={{0,8},{8,16},{32,40},{40,48},{48,56},{64,72},{72,80},{96,104},{104... | collective-permute-start | bytes 393224 | tf_op jit(solution)/shard_map/ppermute | solution.py:291
  36.9 9.5 %collective-permute-start.9 = (bf16[256,256]{1,0:T(8,128)(2,1)S(1)}, bf16[256,256]{1,0:T(8,128)(2,1)S(1)}, u32[]{:S(2)}, u32[]{:S(2)}) collective-permute-start(bf16[256,256]{1,0:T(8,128)(2,1)S(1)} %get-tuple-element.76.refs_1_), channel_id=1, source_target_pairs={{56,64},{120,128},{184,192},{248,256},{312,320},{376,384},{440,448... | collective-permute-start | bytes 393224 | tf_op jit(solution)/shard_map/ppermute | solution.py:293
  40.1 11.2 %collective-permute-start.8 = (bf16[256,256]{1,0:T(8,128)(2,1)S(1)}, bf16[256,256]{1,0:T(8,128)(2,1)S(1)}, u32[]{:S(2)}, u32[]{:S(2)}) collective-permute-start(bf16[256,256]{1,0:T(8,128)(2,1)S(1)} %get-tuple-element.88.refs_1_), channel_id=1, source_target_pairs={{0,8},{8,16},{16,24},{40,48},{48,56},{64,72},{72,80},{80,88},{104,... | collective-permute-start | bytes 393224 | tf_op jit(solution)/shard_map/ppermute | solution.py:291
  44.3 12.1 %collective-permute-start.11 = (bf16[256,256]{1,0:T(8,128)(2,1)S(1)}, bf16[256,256]{1,0:T(8,128)(2,1)S(1)}, u32[]{:S(2)}, u32[]{:S(2)}) collective-permute-start(bf16[256,256]{1,0:T(8,128)(2,1)S(1)} %get-tuple-element.82.refs_1_), channel_id=1, source_target_pairs={{56,64},{120,128},{184,192},{248,256},{312,320},{376,384},{440,448... | collective-permute-start | bytes 393224 | tf_op jit(solution)/shard_map/ppermute | solution.py:293
  52.3 4.1 %collective-permute-start.10 = (bf16[256,256]{1,0:T(8,128)(2,1)S(1)}, bf16[256,256]{1,0:T(8,128)(2,1)S(1)}, u32[]{:S(2)}, u32[]{:S(2)}) collective-permute-start(bf16[256,256]{1,0:T(8,128)(2,1)S(1)} %get-tuple-element.94.refs_1_), channel_id=1, source_target_pairs={{0,8},{8,16},{16,24},{24,32},{48,56},{64,72},{72,80},{80,88},{88,9... | collective-permute-start | bytes 393224 | tf_op jit(solution)/shard_map/ppermute | solution.py:291
  54.3 9.4 %collective-permute-start.13 = (bf16[256,256]{1,0:T(8,128)(2,1)S(1)}, bf16[256,256]{1,0:T(8,128)(2,1)S(1)}, u32[]{:S(2)}, u32[]{:S(2)}) collective-permute-start(bf16[256,256]{1,0:T(8,128)(2,1)S(1)} %get-tuple-element.88.refs_1_), channel_id=1, source_target_pairs={{56,64},{120,128},{184,192},{248,256},{312,320},{376,384},{440,448... | collective-permute-start | bytes 393224 | tf_op jit(solution)/shard_map/ppermute | solution.py:293
  57.5 11.2 %collective-permute-start.12 = (bf16[256,256]{1,0:T(8,128)(2,1)S(1)}, bf16[256,256]{1,0:T(8,128)(2,1)S(1)}, u32[]{:S(2)}, u32[]{:S(2)}) collective-permute-start(bf16[256,256]{1,0:T(8,128)(2,1)S(1)} %get-tuple-element.100.refs_1_), channel_id=1, source_target_pairs={{0,8},{8,16},{16,24},{24,32},{32,40},{64,72},{72,80},{80,88},{88,9... | collective-permute-start | bytes 393224 | tf_op jit(solution)/shard_map/ppermute | solution.py:291
  61.6 11.2 %collective-permute-start.15 = (bf16[256,256]{1,0:T(8,128)(2,1)S(1)}, bf16[256,256]{1,0:T(8,128)(2,1)S(1)}, u32[]{:S(2)}, u32[]{:S(2)}) collective-permute-start(bf16[256,256]{1,0:T(8,128)(2,1)S(1)} %get-tuple-element.94.refs_1_), channel_id=1, source_target_pairs={{56,64},{120,128},{184,192},{248,256},{312,320},{376,384},{440,448... | collective-permute-start | bytes 393224 | tf_op jit(solution)/shard_map/ppermute | solution.py:293
  69.7 4.1 %collective-permute-start.14 = (bf16[256,256]{1,0:T(8,128)(2,1)S(1)}, bf16[256,256]{1,0:T(8,128)(2,1)S(1)}, u32[]{:S(2)}, u32[]{:S(2)}) collective-permute-start(bf16[256,256]{1,0:T(8,128)(2,1)S(1)} %get-tuple-element.106.refs_1_), channel_id=1, source_target_pairs={{0,8},{8,16},{16,24},{24,32},{32,40},{40,48},{64,72},{72,80},{80,8... | collective-permute-start | bytes 393224 | tf_op jit(solution)/shard_map/ppermute | solution.py:291
  71.7 39.2 %copy-start.7 = (s32[8,64]{1,0:T(8,128)S(1)}, s32[8,64]{1,0:T(8,128)}, u32[]{:S(2)}) copy-start(s32[8,64]{1,0:T(8,128)} %plan_ref.1) | copy-start | bytes 6148
  74.9 21.4 %collective-permute-start.16 = (bf16[64,8,128]{2,1,0:T(8,128)(2,1)S(1)}, bf16[64,8,128]{2,1,0:T(8,128)(2,1)}, u32[]{:S(2)}, u32[]{:S(2)}) collective-permute-start(bf16[64,8,128]{2,1,0:T(8,128)(2,1)S(1)} %bitcast.55), channel_id=1, source_target_pairs={{0,1},{1,2},{2,3},{3,4},{4,5},{5,6},{6,7},{7,0},{8,9},{9,10},{10,1... | collective-permute-start | bytes 393224 | tf_op jit(solution)/shard_map/ppermute | solution.py:315
  96.3 29.3 %all-to-all-start = ((bf16[64,8,128]{2,1,0:T(8,128)(2,1)}), bf16[64,8,128]{2,1,0:T(8,128)(2,1)S(1)}, u32[]{:S(2)}, u32[]{:S(2)}) async-start(bf16[64,8,128]{2,1,0:T(8,128)(2,1)} %collective-permute-done.16), calls=%async_computation | async-start | bytes 262144 | tf_op jit(solution)/shard_map/all_to_all | solution.py:316
  127.6 35.9 %all-to-all-start.1 = ((bf16[64,4,8,128]{3,2,1,0:T(8,128)(2,1)}), bf16[64,4,8,128]{3,2,1,0:T(8,128)(2,1)S(1)}, u32[]{:S(2)}, u32[]{:S(2)}) async-start(bf16[64,4,8,128]{3,2,1,0:T(8,128)(2,1)} %shard_map.98), calls=%async_computation.1 | async-start | bytes 1048576 | tf_op jit(solution)/shard_map/all_to_all | solution.py:320
  (3 other events, 4.6 us)
where the time goes:
time: 165 us; the launch traced here: 164 us
  waiting for transfers between devices  82.4 us (50%)
  starting transfers between devices  49.8 us (30%)
  Pallas kernels  29.3 us (18%)
  local copies, waits for them, and re-layouts  1.88 us (1%)
    all_to_all x1, waiting for transfers between devices, shards(): lax.all_to_all(picked, 'blk', split_axis=0, concat_axis=0, tiled=True)  28.3 us
    ppermute x9, waiting for transfers between devices, shards(): arrived = [lax.ppermute(block, 'blk', within), block]  22.9 us
    ppermute x9, starting transfers between devices, shards(): arrived = [lax.ppermute(block, 'blk', within), block]  22.2 us
    ppermute x1, waiting for transfers between devices, shards(): lax.ppermute(pieces, 'group', [(g, (g + 1) % groups) for g in range(group...  18.9 us
    all_to_all x1, starting transfers between devices, shards(): lax.all_to_all(shifted, 'blk', split_axis=0, concat_axis=0, tiled=True)  14.6 us
    all_to_all x1, waiting for transfers between devices, shards(): lax.all_to_all(shifted, 'blk', split_axis=0, concat_axis=0, tiled=True)  12.3 us
    pallas_call x9, Pallas kernels, shards(): call(body, (user_shape, low_shape, rated_shape), [SMEM, SMEM, VMEM, VMEM,...  10.6 us
    pallas_call x9, Pallas kernels, shards(): call(functools.partial(item_body, slot, stops, last, len(arrived)), (piec...  8.63 us
  transfers between devices with their start and end apart: 19, of which 9 were waited for; matrix products, arithmetic and copies ran while one was open for 0% of the time, Pallas kernels for 13%

commit v1 on v0

--- a/solution.py
+++ b/solution.py
@@ -193,7 +193,7 @@
     def _(d):
         filled[d] = 0
         for c in range(CAP):
-            index_ref[d * CAP + c] = -1
+            index_ref[d * CAP + c] = blocks
 
     @pl.loop(0, blocks)
     def _(k):
@@ -203,13 +203,15 @@
         index_ref[dest * CAP + place] = lax.rem(k + (stops - 1), blocks)
 
 
-def pick_body(index_ref, pieces_ref, out_ref):
-    @pl.loop(0, out_ref.shape[0], unroll=8)
+def pick_body(index_ref, pieces_ref, out_ref, held):
+    blocks = pieces_ref.shape[0]
+    held[pl.ds(0, blocks)] = pieces_ref[...]
+    held[blocks] = jnp.zeros(held.shape[1:], held.dtype)
+
+    @pl.loop(0, out_ref.shape[0], unroll=16)
     def _(d):
         for c in range(CAP):
-            at = index_ref[d * CAP + c]
-            piece = pieces_ref[jnp.maximum(at, 0)]
-            out_ref[d, c] = jnp.where(at >= 0, piece, jnp.zeros_like(piece))
+            out_ref[d, c] = held[index_ref[d * CAP + c]]
 
 
 def place_body(pieces_ref, out_ref):
@@ -232,15 +234,6 @@
     items, rank = item_factors.shape[1:]
     wide = tiles_at_stop * tile
     slots = stops + LAG
-
-    index = call(
-        functools.partial(route_body, stops),
-        jax.ShapeDtypeStruct((blocks * CAP,), jnp.int32),
-        [SMEM],
-        SMEM,
-        [pltpu.SMEM((blocks,), jnp.int32)],
-        moved=4 * blocks,
-    )(plan)
 
     low_shape = jax.ShapeDtypeStruct((wide, rank), BF16)
     rated_shape = jax.ShapeDtypeStruct((items, wide), BF16)
@@ -312,10 +305,22 @@
             )(*operands, rating_tiles)
 
     pieces = block.reshape(blocks, -1, 128)
+    index = call(
+        functools.partial(route_body, stops),
+        jax.ShapeDtypeStruct((blocks * CAP,), jnp.int32),
+        [SMEM],
+        SMEM,
+        [pltpu.SMEM((blocks,), jnp.int32)],
+        moved=4 * blocks,
+    )(plan)
     shifted = lax.ppermute(pieces, "group", [(g, (g + 1) % groups) for g in range(groups)])
     spread = lax.all_to_all(shifted, "blk", split_axis=0, concat_axis=0, tiled=True)
     picked = call(
-        pick_body, jax.ShapeDtypeStruct((blocks, CAP) + pieces.shape[1:], BF16), [SMEM, VMEM], VMEM
+        pick_body,
+        jax.ShapeDtypeStruct((blocks, CAP) + pieces.shape[1:], BF16),
+        [SMEM, VMEM],
+        VMEM,
+        [pltpu.VMEM((blocks + 1,) + pieces.shape[1:], BF16)],
     )(index, spread)
     landed = lax.all_to_all(picked, "blk", split_axis=0, concat_axis=0, tiled=True)
     landed = landed.reshape(blocks, CAP, -1, 8, 128).transpose(0, 2, 1, 3, 4)

time: 165 us -> 165 us (level)
  no operation moved by 1% of the time
where the time goes in v1:
time: 165 us; the launch traced here: 164 us
  waiting for transfers between devices  82.4 us (50%)
  starting transfers between devices  49.8 us (30%)
  Pallas kernels  28.9 us (18%)
  local copies, waits for them, and re-layouts  1.88 us (1%)
    all_to_all x1, waiting for transfers between devices, shards(): lax.all_to_all(picked, 'blk', split_axis=0, concat_axis=0, tiled=True)  28.3 us
    ppermute x9, waiting for transfers between devices, shards(): arrived = [lax.ppermute(block, 'blk', within), block]  22.9 us
    ppermute x9, starting transfers between devices, shards(): arrived = [lax.ppermute(block, 'blk', within), block]  22.2 us
    ppermute x1, waiting for transfers between devices, shards(): lax.ppermute(pieces, 'group', [(g, (g + 1) % groups) for g in range(group...  18.9 us
    all_to_all x1, starting transfers between devices, shards(): lax.all_to_all(shifted, 'blk', split_axis=0, concat_axis=0, tiled=True)  14.6 us
    all_to_all x1, waiting for transfers between devices, shards(): lax.all_to_all(shifted, 'blk', split_axis=0, concat_axis=0, tiled=True)  12.3 us
    pallas_call x9, Pallas kernels, shards(): call(body, (user_shape, low_shape, rated_shape), [SMEM, SMEM, VMEM, VMEM,...  10.6 us
    pallas_call x9, Pallas kernels, shards(): call(functools.partial(item_body, slot, stops, last, len(arrived)), (piec...  8.63 us
  transfers between devices with their start and end apart: 19, of which 9 were waited for; matrix products, arithmetic and copies ran while one was open for 0% of the time, Pallas kernels for 13%

profile of v1, /device:TPU:1, one launch (start us, length us, event | category | flops | bytes accessed | tf_op | source)
XLA Modules:
  0.0 164.1 jit_solution(13180821335021102246)
XLA Ops:
  0.7 2.9 %shard_map.77 = (bf16[256,256]{1,0:T(8,128)(2,1)}, bf16[256,512]{1,0:T(8,128)(2,1)}, bf16[256,256]{1,0:T(8,128)(2,1)}) custom-call(s32[8]{0:T(128)} %bitcast.24, s32[2,8]{1,0:T(2,128)} %bitcast.44, f32[1024,256]{1,0:T(8,128)} %bitcast.21, f32[256,256]{1,0:T(8,128)} %bitcast.58, bf16[8,2,256,256]{3,2,1,0:T(8,128)(2,1)} %bitcast.11), custom_call_target="tpu_custom_call" | custom-call | flops 134217728 | bytes 1048576 | tf_op jit(solution)/shard_map/pallas_call | solution.py:244
  3.6 4.4 %collective-permute-start = (bf16[256,256]{1,0:T(8,128)(2,1)}, bf16[256,256]{1,0:T(8,128)(2,1)S(1)}, u32[]{:S(2)}, u32[]{:S(2)}) collective-permute-start(bf16[256,256]{1,0:T(8,128)(2,1)} %get-tuple-element.59.refs_1_), channel_id=1, source_target_pairs={{0,8},{8,16},{16,24},{24,32},{32,40},{40,48},{48,56},{64,72},{72,8... | collective-permute-start | bytes 393224 | tf_op jit(solution)/shard_map/ppermute | solution.py:284
  11.1 1.5 collective-permute-done.refs_0_
  13.7 1.8 %collective-permute-start.1 = (bf16[256,256]{1,0:T(8,128)(2,1)S(1)}, bf16[256,256]{1,0:T(8,128)(2,1)S(1)}, u32[]{:S(2)}, u32[]{:S(2)}) collective-permute-start(bf16[256,256]{1,0:T(8,128)(2,1)S(1)} %get-tuple-element.64.refs_1_), channel_id=1, source_target_pairs={{8,16},{16,24},{24,32},{32,40},{40,48},{48,56},{72,80},{80,88},{88... | collective-permute-start | bytes 393224 | tf_op jit(solution)/shard_map/ppermute | solution.py:284
  23.7 10.2 %collective-permute-done.4.refs_0_ = bf16[256,256]{1,0:T(8,128)(2,1)S(1)} collective-permute-done((bf16[256,256]{1,0:T(8,128)(2,1)S(1)}, bf16[256,256]{1,0:T(8,128)(2,1)S(1)}, u32[]{:S(2)}, u32[]{:S(2)}) %collective-permute-start.4) | collective-permute-done | bytes 131104 | tf_op jit(solution)/shard_map/ppermute | solution.py:284
  35.0 1.9 %collective-permute-start.6 = (bf16[256,256]{1,0:T(8,128)(2,1)S(1)}, bf16[256,256]{1,0:T(8,128)(2,1)S(1)}, u32[]{:S(2)}, u32[]{:S(2)}) collective-permute-start(bf16[256,256]{1,0:T(8,128)(2,1)S(1)} %get-tuple-element.82.refs_1_), channel_id=1, source_target_pairs={{0,8},{8,16},{32,40},{40,48},{48,56},{64,72},{72,80},{96,104},{104... | collective-permute-start | bytes 393224 | tf_op jit(solution)/shard_map/ppermute | solution.py:284
  37.6 1.4 shard_map.86
  40.1 4.1 %collective-permute-start.8 = (bf16[256,256]{1,0:T(8,128)(2,1)S(1)}, bf16[256,256]{1,0:T(8,128)(2,1)S(1)}, u32[]{:S(2)}, u32[]{:S(2)}) collective-permute-start(bf16[256,256]{1,0:T(8,128)(2,1)S(1)} %get-tuple-element.88.refs_1_), channel_id=1, source_target_pairs={{0,8},{8,16},{16,24},{40,48},{48,56},{64,72},{72,80},{80,88},{104,... | collective-permute-start | bytes 393224 | tf_op jit(solution)/shard_map/ppermute | solution.py:284
  44.9 1.4 shard_map.88
  46.4 4.9 %collective-permute-done.8.refs_0_ = bf16[256,256]{1,0:T(8,128)(2,1)S(1)} collective-permute-done((bf16[256,256]{1,0:T(8,128)(2,1)S(1)}, bf16[256,256]{1,0:T(8,128)(2,1)S(1)}, u32[]{:S(2)}, u32[]{:S(2)}) %collective-permute-start.8) | collective-permute-done | bytes 131104 | tf_op jit(solution)/shard_map/ppermute | solution.py:284
  52.3 1.9 %collective-permute-start.10 = (bf16[256,256]{1,0:T(8,128)(2,1)S(1)}, bf16[256,256]{1,0:T(8,128)(2,1)S(1)}, u32[]{:S(2)}, u32[]{:S(2)}) collective-permute-start(bf16[256,256]{1,0:T(8,128)(2,1)S(1)} %get-tuple-element.94.refs_1_), channel_id=1, source_target_pairs={{0,8},{8,16},{16,24},{24,32},{48,56},{64,72},{72,80},{80,88},{88,9... | collective-permute-start | bytes 393224 | tf_op jit(solution)/shard_map/ppermute | solution.py:284
  55.0 1.4 shard_map.90
  57.5 4.1 %collective-permute-start.12 = (bf16[256,256]{1,0:T(8,128)(2,1)S(1)}, bf16[256,256]{1,0:T(8,128)(2,1)S(1)}, u32[]{:S(2)}, u32[]{:S(2)}) collective-permute-start(bf16[256,256]{1,0:T(8,128)(2,1)S(1)} %get-tuple-element.100.refs_1_), channel_id=1, source_target_pairs={{0,8},{8,16},{16,24},{24,32},{32,40},{64,72},{72,80},{80,88},{88,9... | collective-permute-start | bytes 393224 | tf_op jit(solution)/shard_map/ppermute | solution.py:284
  63.7 5.0 %collective-permute-done.12.refs_0_ = bf16[256,256]{1,0:T(8,128)(2,1)S(1)} collective-permute-done((bf16[256,256]{1,0:T(8,128)(2,1)S(1)}, bf16[256,256]{1,0:T(8,128)(2,1)S(1)}, u32[]{:S(2)}, u32[]{:S(2)}) %collective-permute-start.12) | collective-permute-done | bytes 131104 | tf_op jit(solution)/shard_map/ppermute | solution.py:284
  69.7 1.9 %collective-permute-start.14 = (bf16[256,256]{1,0:T(8,128)(2,1)S(1)}, bf16[256,256]{1,0:T(8,128)(2,1)S(1)}, u32[]{:S(2)}, u32[]{:S(2)}) collective-permute-start(bf16[256,256]{1,0:T(8,128)(2,1)S(1)} %get-tuple-element.106.refs_1_), channel_id=1, source_target_pairs={{0,8},{8,16},{16,24},{24,32},{32,40},{40,48},{64,72},{72,80},{80,8... | collective-permute-start | bytes 393224 | tf_op jit(solution)/shard_map/ppermute | solution.py:284
  74.9 2.5 %collective-permute-start.16 = (bf16[64,8,128]{2,1,0:T(8,128)(2,1)S(1)}, bf16[64,8,128]{2,1,0:T(8,128)(2,1)}, u32[]{:S(2)}, u32[]{:S(2)}) collective-permute-start(bf16[64,8,128]{2,1,0:T(8,128)(2,1)S(1)} %bitcast.55), channel_id=1, source_target_pairs={{0,1},{1,2},{2,3},{3,4},{4,5},{5,6},{6,7},{7,0},{8,9},{9,10},{10,1... | collective-permute-start | bytes 393224 | tf_op jit(solution)/shard_map/ppermute | solution.py:316
  77.4 18.9 %collective-permute-done.16 = bf16[64,8,128]{2,1,0:T(8,128)(2,1)} collective-permute-done((bf16[64,8,128]{2,1,0:T(8,128)(2,1)S(1)}, bf16[64,8,128]{2,1,0:T(8,128)(2,1)}, u32[]{:S(2)}, u32[]{:S(2)}) %collective-permute-start.16) | collective-permute-done | bytes 131104 | tf_op jit(solution)/shard_map/ppermute | solution.py:316
  96.3 14.6 %all-to-all-start = ((bf16[64,8,128]{2,1,0:T(8,128)(2,1)}), bf16[64,8,128]{2,1,0:T(8,128)(2,1)S(1)}, u32[]{:S(2)}, u32[]{:S(2)}) async-start(bf16[64,8,128]{2,1,0:T(8,128)(2,1)} %collective-permute-done.16), calls=%async_computation | async-start | bytes 262144 | tf_op jit(solution)/shard_map/all_to_all | solution.py:317
  110.9 2.4 %shard_map.97.index_ref = s32[256]{0:T(256)S(1)} custom-call(s32[8,64]{1,0:T(8,128)S(1)} %copy-done.7), custom_call_target="tpu_custom_call" | custom-call | bytes 256 | tf_op jit(solution)/shard_map/pallas_call | solution.py:308
  113.3 12.3 %all-to-all-done.pieces_ref = bf16[64,8,128]{2,1,0:T(8,128)(2,1)S(1)} async-done(((bf16[64,8,128]{2,1,0:T(8,128)(2,1)}), bf16[64,8,128]{2,1,0:T(8,128)(2,1)S(1)}, u32[]{:S(2)}, u32[]{:S(2)}) %all-to-all-start) | async-done | bytes 131104 | tf_op jit(solution)/shard_map/all_to_all | solution.py:317
  125.6 1.6 shard_map.98
  127.3 5.7 %all-to-all-start.1 = ((bf16[64,4,8,128]{3,2,1,0:T(8,128)(2,1)}), bf16[64,4,8,128]{3,2,1,0:T(8,128)(2,1)S(1)}, u32[]{:S(2)}, u32[]{:S(2)}) async-start(bf16[64,4,8,128]{3,2,1,0:T(8,128)(2,1)} %shard_map.98), calls=%async_computation.1 | async-start | bytes 1048576 | tf_op jit(solution)/shard_map/all_to_all | solution.py:325
  133.0 1.8 %shard_map.96 = f32[1024,256]{1,0:T(8,128)} custom-call(s32[8]{0:T(128)S(1)} %bitcast.43, s32[2,8]{1,0:T(2,128)S(1)} %bitcast.54, bf16[256,512]{1,0:T(8,128)(2,1)S(1)} %get-tuple-element.112.residual_ref, bf16[256,256]{1,0:T(8,128)(2,1)S(1)} %get-tuple-element.113.item_ref, f32[1024,256]{1,0:T(8,128)S(1)} %get-tuple-element.114.user_ref), custom_call_target="tpu_custom_call" | custom-call | flops 67108864 | bytes 1048576 | tf_op jit(solution)/shard_map/pallas_call | solution.py:293
  134.8 28.3 %all-to-all-done.1 = bf16[64,4,8,128]{3,2,1,0:T(8,128)(2,1)S(1)} async-done(((bf16[64,4,8,128]{3,2,1,0:T(8,128)(2,1)}), bf16[64,4,8,128]{3,2,1,0:T(8,128)(2,1)S(1)}, u32[]{:S(2)}, u32[]{:S(2)}) %all-to-all-start.1) | async-done | bytes 524320 | tf_op jit(solution)/shard_map/all_to_all | solution.py:325
  (53 shorter events, 25.7 us)
Async XLA Ops:
  0.6 7.4 %copy-start.3 = (s32[1,1,8]{2,1,0:T(1,128)S(1)}, s32[1,1,8]{2,1,0:T(1,128)}, u32[]{:S(2)}) copy-start(s32[1,1,8]{2,1,0:T(1,128)} %param.10) | copy-start | bytes 100
  0.6 7.4 %copy-start.6 = (s32[1,1,8,2]{2,3,1,0:T(2,128)S(1)}, s32[1,1,8,2]{2,3,1,0:T(2,128)}, u32[]{:S(2)}) copy-start(s32[1,1,8,2]{2,3,1,0:T(2,128)} %param.9) | copy-start | bytes 196
  0.7 7.4 %copy-start = (bf16[1,1,8,2,256,256]{5,4,3,2,1,0:T(8,128)(2,1)S(1)}, bf16[1,1,8,2,256,256]{5,4,3,2,1,0:T(8,128)(2,1)}, u32[]{:S(2)}) copy-start(bf16[1,1,8,2,256,256]{5,4,3,2,1,0:T(8,128)(2,1)} %param.8) | copy-start | bytes 6291460
  0.7 7.4 %copy-start.1 = (f32[1,1024,256]{2,1,0:T(8,128)S(1)}, f32[1,1024,256]{2,1,0:T(8,128)}, u32[]{:S(2)}) copy-start(f32[1,1024,256]{2,1,0:T(8,128)} %param.6) | copy-start | bytes 3145732
  3.6 9.1 %collective-permute-start = (bf16[256,256]{1,0:T(8,128)(2,1)}, bf16[256,256]{1,0:T(8,128)(2,1)S(1)}, u32[]{:S(2)}, u32[]{:S(2)}) collective-permute-start(bf16[256,256]{1,0:T(8,128)(2,1)} %get-tuple-element.59.refs_1_), channel_id=1, source_target_pairs={{0,8},{8,16},{16,24},{24,32},{32,40},{40,48},{48,56},{64,72},{72,8... | collective-permute-start | bytes 393224 | tf_op jit(solution)/shard_map/ppermute | solution.py:284
  13.7 3.8 %collective-permute-start.1 = (bf16[256,256]{1,0:T(8,128)(2,1)S(1)}, bf16[256,256]{1,0:T(8,128)(2,1)S(1)}, u32[]{:S(2)}, u32[]{:S(2)}) collective-permute-start(bf16[256,256]{1,0:T(8,128)(2,1)S(1)} %get-tuple-element.64.refs_1_), channel_id=1, source_target_pairs={{8,16},{16,24},{24,32},{32,40},{40,48},{48,56},{72,80},{80,88},{88... | collective-permute-start | bytes 393224 | tf_op jit(solution)/shard_map/ppermute | solution.py:284
  15.6 4.6 %collective-permute-start.3 = (bf16[256,256]{1,0:T(8,128)(2,1)S(1)}, bf16[256,256]{1,0:T(8,128)(2,1)S(1)}, u32[]{:S(2)}, u32[]{:S(2)}) collective-permute-start(bf16[256,256]{1,0:T(8,128)(2,1)S(1)} %copy-done.5), channel_id=1, source_target_pairs={{56,64},{120,128},{184,192},{248,256},{312,320},{376,384},{440,448... | collective-permute-start | bytes 393224 | tf_op jit(solution)/shard_map/ppermute | solution.py:286
  18.1 2.1 %collective-permute-start.2 = (bf16[256,256]{1,0:T(8,128)(2,1)S(1)}, bf16[256,256]{1,0:T(8,128)(2,1)S(1)}, u32[]{:S(2)}, u32[]{:S(2)}) collective-permute-start(bf16[256,256]{1,0:T(8,128)(2,1)S(1)} %get-tuple-element.70.refs_1_), channel_id=1, source_target_pairs={{16,24},{24,32},{32,40},{40,48},{48,56},{80,88},{88,96},{96,104},{... | collective-permute-start | bytes 393224 | tf_op jit(solution)/shard_map/ppermute | solution.py:284
  18.7 5.0 %collective-permute-start.5 = (bf16[256,256]{1,0:T(8,128)(2,1)S(1)}, bf16[256,256]{1,0:T(8,128)(2,1)S(1)}, u32[]{:S(2)}, u32[]{:S(2)}) collective-permute-start(bf16[256,256]{1,0:T(8,128)(2,1)S(1)} %get-tuple-element.64.refs_1_), channel_id=1, source_target_pairs={{56,64},{120,128},{184,192},{248,256},{312,320},{376,384},{440,448... | collective-permute-start | bytes 393224 | tf_op jit(solution)/shard_map/ppermute | solution.py:286
  20.8 13.1 %collective-permute-start.4 = (bf16[256,256]{1,0:T(8,128)(2,1)S(1)}, bf16[256,256]{1,0:T(8,128)(2,1)S(1)}, u32[]{:S(2)}, u32[]{:S(2)}) collective-permute-start(bf16[256,256]{1,0:T(8,128)(2,1)S(1)} %get-tuple-element.76.refs_1_), channel_id=1, source_target_pairs={{0,8},{24,32},{32,40},{40,48},{48,56},{64,72},{88,96},{96,104},{10... | collective-permute-start | bytes 393224 | tf_op jit(solution)/shard_map/ppermute | solution.py:284
  22.1 17.0 %collective-permute-start.7 = (bf16[256,256]{1,0:T(8,128)(2,1)S(1)}, bf16[256,256]{1,0:T(8,128)(2,1)S(1)}, u32[]{:S(2)}, u32[]{:S(2)}) collective-permute-start(bf16[256,256]{1,0:T(8,128)(2,1)S(1)} %get-tuple-element.70.refs_1_), channel_id=1, source_target_pairs={{56,64},{120,128},{184,192},{248,256},{312,320},{376,384},{440,448... | collective-permute-start | bytes 393224 | tf_op jit(solution)/shard_map/ppermute | solution.py:286
  35.0 4.1 %collective-permute-start.6 = (bf16[256,256]{1,0:T(8,128)(2,1)S(1)}, bf16[256,256]{1,0:T(8,128)(2,1)S(1)}, u32[]{:S(2)}, u32[]{:S(2)}) collective-permute-start(bf16[256,256]{1,0:T(8,128)(2,1)S(1)} %get-tuple-element.82.refs_1_), channel_id=1, source_target_pairs={{0,8},{8,16},{32,40},{40,48},{48,56},{64,72},{72,80},{96,104},{104... | collective-permute-start | bytes 393224 | tf_op jit(solution)/shard_map/ppermute | solution.py:284
  36.9 9.5 %collective-permute-start.9 = (bf16[256,256]{1,0:T(8,128)(2,1)S(1)}, bf16[256,256]{1,0:T(8,128)(2,1)S(1)}, u32[]{:S(2)}, u32[]{:S(2)}) collective-permute-start(bf16[256,256]{1,0:T(8,128)(2,1)S(1)} %get-tuple-element.76.refs_1_), channel_id=1, source_target_pairs={{56,64},{120,128},{184,192},{248,256},{312,320},{376,384},{440,448... | collective-permute-start | bytes 393224 | tf_op jit(solution)/shard_map/ppermute | solution.py:286
  40.1 11.2 %collective-permute-start.8 = (bf16[256,256]{1,0:T(8,128)(2,1)S(1)}, bf16[256,256]{1,0:T(8,128)(2,1)S(1)}, u32[]{:S(2)}, u32[]{:S(2)}) collective-permute-start(bf16[256,256]{1,0:T(8,128)(2,1)S(1)} %get-tuple-element.88.refs_1_), channel_id=1, source_target_pairs={{0,8},{8,16},{16,24},{40,48},{48,56},{64,72},{72,80},{80,88},{104,... | collective-permute-start | bytes 393224 | tf_op jit(solution)/shard_map/ppermute | solution.py:284
  44.3 12.1 %collective-permute-start.11 = (bf16[256,256]{1,0:T(8,128)(2,1)S(1)}, bf16[256,256]{1,0:T(8,128)(2,1)S(1)}, u32[]{:S(2)}, u32[]{:S(2)}) collective-permute-start(bf16[256,256]{1,0:T(8,128)(2,1)S(1)} %get-tuple-element.82.refs_1_), channel_id=1, source_target_pairs={{56,64},{120,128},{184,192},{248,256},{312,320},{376,384},{440,448... | collective-permute-start | bytes 393224 | tf_op jit(solution)/shard_map/ppermute | solution.py:286
  52.3 4.1 %collective-permute-start.10 = (bf16[256,256]{1,0:T(8,128)(2,1)S(1)}, bf16[256,256]{1,0:T(8,128)(2,1)S(1)}, u32[]{:S(2)}, u32[]{:S(2)}) collective-permute-start(bf16[256,256]{1,0:T(8,128)(2,1)S(1)} %get-tuple-element.94.refs_1_), channel_id=1, source_target_pairs={{0,8},{8,16},{16,24},{24,32},{48,56},{64,72},{72,80},{80,88},{88,9... | collective-permute-start | bytes 393224 | tf_op jit(solution)/shard_map/ppermute | solution.py:284
  54.3 9.4 %collective-permute-start.13 = (bf16[256,256]{1,0:T(8,128)(2,1)S(1)}, bf16[256,256]{1,0:T(8,128)(2,1)S(1)}, u32[]{:S(2)}, u32[]{:S(2)}) collective-permute-start(bf16[256,256]{1,0:T(8,128)(2,1)S(1)} %get-tuple-element.88.refs_1_), channel_id=1, source_target_pairs={{56,64},{120,128},{184,192},{248,256},{312,320},{376,384},{440,448... | collective-permute-start | bytes 393224 | tf_op jit(solution)/shard_map/ppermute | solution.py:286
  57.5 11.2 %collective-permute-start.12 = (bf16[256,256]{1,0:T(8,128)(2,1)S(1)}, bf16[256,256]{1,0:T(8,128)(2,1)S(1)}, u32[]{:S(2)}, u32[]{:S(2)}) collective-permute-start(bf16[256,256]{1,0:T(8,128)(2,1)S(1)} %get-tuple-element.100.refs_1_), channel_id=1, source_target_pairs={{0,8},{8,16},{16,24},{24,32},{32,40},{64,72},{72,80},{80,88},{88,9... | collective-permute-start | bytes 393224 | tf_op jit(solution)/shard_map/ppermute | solution.py:284
  61.6 11.2 %collective-permute-start.15 = (bf16[256,256]{1,0:T(8,128)(2,1)S(1)}, bf16[256,256]{1,0:T(8,128)(2,1)S(1)}, u32[]{:S(2)}, u32[]{:S(2)}) collective-permute-start(bf16[256,256]{1,0:T(8,128)(2,1)S(1)} %get-tuple-element.94.refs_1_), channel_id=1, source_target_pairs={{56,64},{120,128},{184,192},{248,256},{312,320},{376,384},{440,448... | collective-permute-start | bytes 393224 | tf_op jit(solution)/shard_map/ppermute | solution.py:286
  69.7 4.1 %collective-permute-start.14 = (bf16[256,256]{1,0:T(8,128)(2,1)S(1)}, bf16[256,256]{1,0:T(8,128)(2,1)S(1)}, u32[]{:S(2)}, u32[]{:S(2)}) collective-permute-start(bf16[256,256]{1,0:T(8,128)(2,1)S(1)} %get-tuple-element.106.refs_1_), channel_id=1, source_target_pairs={{0,8},{8,16},{16,24},{24,32},{32,40},{40,48},{64,72},{72,80},{80,8... | collective-permute-start | bytes 393224 | tf_op jit(solution)/shard_map/ppermute | solution.py:284
  71.7 39.2 %copy-start.7 = (s32[8,64]{1,0:T(8,128)S(1)}, s32[8,64]{1,0:T(8,128)}, u32[]{:S(2)}) copy-start(s32[8,64]{1,0:T(8,128)} %plan_ref.1) | copy-start | bytes 6148
  74.9 21.4 %collective-permute-start.16 = (bf16[64,8,128]{2,1,0:T(8,128)(2,1)S(1)}, bf16[64,8,128]{2,1,0:T(8,128)(2,1)}, u32[]{:S(2)}, u32[]{:S(2)}) collective-permute-start(bf16[64,8,128]{2,1,0:T(8,128)(2,1)S(1)} %bitcast.55), channel_id=1, source_target_pairs={{0,1},{1,2},{2,3},{3,4},{4,5},{5,6},{6,7},{7,0},{8,9},{9,10},{10,1... | collective-permute-start | bytes 393224 | tf_op jit(solution)/shard_map/ppermute | solution.py:316
  96.3 29.3 %all-to-all-start = ((bf16[64,8,128]{2,1,0:T(8,128)(2,1)}), bf16[64,8,128]{2,1,0:T(8,128)(2,1)S(1)}, u32[]{:S(2)}, u32[]{:S(2)}) async-start(bf16[64,8,128]{2,1,0:T(8,128)(2,1)} %collective-permute-done.16), calls=%async_computation | async-start | bytes 262144 | tf_op jit(solution)/shard_map/all_to_all | solution.py:317
  127.3 35.9 %all-to-all-start.1 = ((bf16[64,4,8,128]{3,2,1,0:T(8,128)(2,1)}), bf16[64,4,8,128]{3,2,1,0:T(8,128)(2,1)S(1)}, u32[]{:S(2)}, u32[]{:S(2)}) async-start(bf16[64,4,8,128]{3,2,1,0:T(8,128)(2,1)} %shard_map.98), calls=%async_computation.1 | async-start | bytes 1048576 | tf_op jit(solution)/shard_map/all_to_all | solution.py:325
  (3 other events, 4.6 us)

commit v2 on v1

--- a/solution.py
+++ b/solution.py
@@ -10,6 +10,7 @@
 
 CAP = 4
 PLANE = 8
+GROUP_ROW = 4
 LAG = 2
 
 
@@ -40,6 +41,13 @@
         cost_estimate=pl.CostEstimate(flops=flops, bytes_accessed=moved, transcendentals=0),
         compiler_params=pltpu.CompilerParams(vmem_limit_bytes=limit),
     )
+
+
+def hand_over(position, group, blocks, groups):
+    if group % GROUP_ROW == GROUP_ROW - 1:
+        plane, inner = divmod(position, PLANE)
+        position = (blocks // PLANE - 1 - plane) * PLANE + inner
+    return position, (group + 1) % groups
 
 
 def stop_at(slot, inner, stops):
@@ -188,6 +196,7 @@
 def route_body(stops, plan_ref, index_ref, filled):
     groups, blocks = plan_ref.shape
     group = lax.rem(lax.axis_index("group") + groups - 1, groups)
+    turned = lax.rem(group, GROUP_ROW) == GROUP_ROW - 1
 
     @pl.loop(0, blocks)
     def _(d):
@@ -200,7 +209,9 @@
         dest = plan_ref[group, k]
         place = filled[dest]
         filled[dest] = place + 1
-        index_ref[dest * CAP + place] = lax.rem(k + (stops - 1), blocks)
+        at = lax.rem(k + (stops - 1), blocks)
+        inner = lax.rem(at, PLANE)
+        index_ref[dest * CAP + place] = jnp.where(turned, blocks - PLANE - at + 2 * inner, at)
 
 
 def pick_body(index_ref, pieces_ref, out_ref, held):
@@ -313,7 +324,12 @@
         [pltpu.SMEM((blocks,), jnp.int32)],
         moved=4 * blocks,
     )(plan)
-    shifted = lax.ppermute(pieces, "group", [(g, (g + 1) % groups) for g in range(groups)])
+    moves = []
+    for b in range(blocks):
+        for g in range(groups):
+            to_b, to_g = hand_over(b, g, blocks, groups)
+            moves.append((b * groups + g, to_b * groups + to_g))
+    shifted = lax.ppermute(pieces, ("blk", "group"), moves)
     spread = lax.all_to_all(shifted, "blk", split_axis=0, concat_axis=0, tiled=True)
     picked = call(
         pick_body,

time: 165 us -> 160 us (0.970)
  waiting for transfers between devices: 82.4 us -> 72.5 us
  starting transfers between devices: 49.8 us -> 54.9 us
    ppermute x1, waiting for transfers between devices: 18.9 us -> 9.22 us  [shards(): shifted = lax.ppermute(pieces, ('blk', 'group'), moves)]
    all_to_all x1, starting transfers between devices: 14.6 us -> 19.7 us  [shards(): lax.all_to_all(shifted, 'blk', split_axis=0, concat_axis=0, tiled=True)]
where the time goes in v2:
time: 160 us; the launch traced here: 159 us
  waiting for transfers between devices  72.5 us (45%)
  starting transfers between devices  54.9 us (34%)
  Pallas kernels  29 us (18%)
  local copies, waits for them, and re-layouts  1.88 us (1%)
    all_to_all x1, waiting for transfers between devices, shards(): lax.all_to_all(picked, 'blk', split_axis=0, concat_axis=0, tiled=True)  28.3 us
    ppermute x9, waiting for transfers between devices, shards(): arrived = [lax.ppermute(block, 'blk', within), block]  22.9 us
    ppermute x9, starting transfers between devices, shards(): arrived = [lax.ppermute(block, 'blk', within), block]  22.2 us
    all_to_all x1, starting transfers between devices, shards(): lax.all_to_all(shifted, 'blk', split_axis=0, concat_axis=0, tiled=True)  19.7 us
    all_to_all x1, waiting for transfers between devices, shards(): lax.all_to_all(shifted, 'blk', split_axis=0, concat_axis=0, tiled=True)  12.1 us
    pallas_call x9, Pallas kernels, shards(): call(body, (user_shape, low_shape, rated_shape), [SMEM, SMEM, VMEM, VMEM,...  10.6 us
    ppermute x1, waiting for transfers between devices, shards(): shifted = lax.ppermute(pieces, ('blk', 'group'), moves)  9.22 us
    pallas_call x9, Pallas kernels, shards(): call(functools.partial(item_body, slot, stops, last, len(arrived)), (piec...  8.63 us
  transfers between devices with their start and end apart: 19, of which 9 were waited for; matrix products, arithmetic and copies ran while one was open for 0% of the time, Pallas kernels for 13%

profile of v2, /device:TPU:1, one launch (start us, length us, event | category | flops | bytes accessed | tf_op | source)
XLA Modules:
  0.0 159.4 jit_solution(13914081555727664913)
XLA Ops:
  0.7 2.9 %shard_map.77 = (bf16[256,256]{1,0:T(8,128)(2,1)}, bf16[256,512]{1,0:T(8,128)(2,1)}, bf16[256,256]{1,0:T(8,128)(2,1)}) custom-call(s32[8]{0:T(128)} %bitcast.24, s32[2,8]{1,0:T(2,128)} %bitcast.44, f32[1024,256]{1,0:T(8,128)} %bitcast.21, f32[256,256]{1,0:T(8,128)} %bitcast.58, bf16[8,2,256,256]{3,2,1,0:T(8,128)(2,1)} %bitcast.11), custom_call_target="tpu_custom_call" | custom-call | flops 134217728 | bytes 1048576 | tf_op jit(solution)/shard_map/pallas_call | solution.py:255
  3.6 4.4 %collective-permute-start = (bf16[256,256]{1,0:T(8,128)(2,1)}, bf16[256,256]{1,0:T(8,128)(2,1)S(1)}, u32[]{:S(2)}, u32[]{:S(2)}) collective-permute-start(bf16[256,256]{1,0:T(8,128)(2,1)} %get-tuple-element.59.refs_1_), channel_id=1, source_target_pairs={{0,8},{8,16},{16,24},{24,32},{32,40},{40,48},{48,56},{64,72},{72,8... | collective-permute-start | bytes 393224 | tf_op jit(solution)/shard_map/ppermute | solution.py:295
  11.1 1.5 collective-permute-done.refs_0_
  13.7 1.8 %collective-permute-start.1 = (bf16[256,256]{1,0:T(8,128)(2,1)S(1)}, bf16[256,256]{1,0:T(8,128)(2,1)S(1)}, u32[]{:S(2)}, u32[]{:S(2)}) collective-permute-start(bf16[256,256]{1,0:T(8,128)(2,1)S(1)} %get-tuple-element.64.refs_1_), channel_id=1, source_target_pairs={{8,16},{16,24},{24,32},{32,40},{40,48},{48,56},{72,80},{80,88},{88... | collective-permute-start | bytes 393224 | tf_op jit(solution)/shard_map/ppermute | solution.py:295
  23.7 10.2 %collective-permute-done.4.refs_0_ = bf16[256,256]{1,0:T(8,128)(2,1)S(1)} collective-permute-done((bf16[256,256]{1,0:T(8,128)(2,1)S(1)}, bf16[256,256]{1,0:T(8,128)(2,1)S(1)}, u32[]{:S(2)}, u32[]{:S(2)}) %collective-permute-start.4) | collective-permute-done | bytes 131104 | tf_op jit(solution)/shard_map/ppermute | solution.py:295
  35.0 1.9 %collective-permute-start.6 = (bf16[256,256]{1,0:T(8,128)(2,1)S(1)}, bf16[256,256]{1,0:T(8,128)(2,1)S(1)}, u32[]{:S(2)}, u32[]{:S(2)}) collective-permute-start(bf16[256,256]{1,0:T(8,128)(2,1)S(1)} %get-tuple-element.82.refs_1_), channel_id=1, source_target_pairs={{0,8},{8,16},{32,40},{40,48},{48,56},{64,72},{72,80},{96,104},{104... | collective-permute-start | bytes 393224 | tf_op jit(solution)/shard_map/ppermute | solution.py:295
  37.6 1.4 shard_map.86
  40.1 4.1 %collective-permute-start.8 = (bf16[256,256]{1,0:T(8,128)(2,1)S(1)}, bf16[256,256]{1,0:T(8,128)(2,1)S(1)}, u32[]{:S(2)}, u32[]{:S(2)}) collective-permute-start(bf16[256,256]{1,0:T(8,128)(2,1)S(1)} %get-tuple-element.88.refs_1_), channel_id=1, source_target_pairs={{0,8},{8,16},{16,24},{40,48},{48,56},{64,72},{72,80},{80,88},{104,... | collective-permute-start | bytes 393224 | tf_op jit(solution)/shard_map/ppermute | solution.py:295
  44.9 1.4 shard_map.88
  46.4 4.9 %collective-permute-done.8.refs_0_ = bf16[256,256]{1,0:T(8,128)(2,1)S(1)} collective-permute-done((bf16[256,256]{1,0:T(8,128)(2,1)S(1)}, bf16[256,256]{1,0:T(8,128)(2,1)S(1)}, u32[]{:S(2)}, u32[]{:S(2)}) %collective-permute-start.8) | collective-permute-done | bytes 131104 | tf_op jit(solution)/shard_map/ppermute | solution.py:295
  52.3 1.9 %collective-permute-start.10 = (bf16[256,256]{1,0:T(8,128)(2,1)S(1)}, bf16[256,256]{1,0:T(8,128)(2,1)S(1)}, u32[]{:S(2)}, u32[]{:S(2)}) collective-permute-start(bf16[256,256]{1,0:T(8,128)(2,1)S(1)} %get-tuple-element.94.refs_1_), channel_id=1, source_target_pairs={{0,8},{8,16},{16,24},{24,32},{48,56},{64,72},{72,80},{80,88},{88,9... | collective-permute-start | bytes 393224 | tf_op jit(solution)/shard_map/ppermute | solution.py:295
  55.0 1.4 shard_map.90
  57.5 4.1 %collective-permute-start.12 = (bf16[256,256]{1,0:T(8,128)(2,1)S(1)}, bf16[256,256]{1,0:T(8,128)(2,1)S(1)}, u32[]{:S(2)}, u32[]{:S(2)}) collective-permute-start(bf16[256,256]{1,0:T(8,128)(2,1)S(1)} %get-tuple-element.100.refs_1_), channel_id=1, source_target_pairs={{0,8},{8,16},{16,24},{24,32},{32,40},{64,72},{72,80},{80,88},{88,9... | collective-permute-start | bytes 393224 | tf_op jit(solution)/shard_map/ppermute | solution.py:295
  63.7 5.0 %collective-permute-done.12.refs_0_ = bf16[256,256]{1,0:T(8,128)(2,1)S(1)} collective-permute-done((bf16[256,256]{1,0:T(8,128)(2,1)S(1)}, bf16[256,256]{1,0:T(8,128)(2,1)S(1)}, u32[]{:S(2)}, u32[]{:S(2)}) %collective-permute-start.12) | collective-permute-done | bytes 131104 | tf_op jit(solution)/shard_map/ppermute | solution.py:295
  69.7 1.9 %collective-permute-start.14 = (bf16[256,256]{1,0:T(8,128)(2,1)S(1)}, bf16[256,256]{1,0:T(8,128)(2,1)S(1)}, u32[]{:S(2)}, u32[]{:S(2)}) collective-permute-start(bf16[256,256]{1,0:T(8,128)(2,1)S(1)} %get-tuple-element.106.refs_1_), channel_id=1, source_target_pairs={{0,8},{8,16},{16,24},{24,32},{32,40},{40,48},{64,72},{72,80},{80,8... | collective-permute-start | bytes 393224 | tf_op jit(solution)/shard_map/ppermute | solution.py:295
  74.9 2.5 %collective-permute-start.16 = (bf16[64,8,128]{2,1,0:T(8,128)(2,1)S(1)}, bf16[64,8,128]{2,1,0:T(8,128)(2,1)}, u32[]{:S(2)}, u32[]{:S(2)}) collective-permute-start(bf16[64,8,128]{2,1,0:T(8,128)(2,1)S(1)} %bitcast.55), channel_id=1, source_target_pairs={{0,1},{1,2},{2,3},{3,452},{4,5},{5,6},{6,7},{7,448},{8,9},{9,10},{... | collective-permute-start | bytes 393224 | tf_op jit(solution)/shard_map/ppermute | solution.py:332
  77.4 9.2 %collective-permute-done.16 = bf16[64,8,128]{2,1,0:T(8,128)(2,1)} collective-permute-done((bf16[64,8,128]{2,1,0:T(8,128)(2,1)S(1)}, bf16[64,8,128]{2,1,0:T(8,128)(2,1)}, u32[]{:S(2)}, u32[]{:S(2)}) %collective-permute-start.16) | collective-permute-done | bytes 131104 | tf_op jit(solution)/shard_map/ppermute | solution.py:332
  86.6 19.7 %all-to-all-start = ((bf16[64,8,128]{2,1,0:T(8,128)(2,1)}), bf16[64,8,128]{2,1,0:T(8,128)(2,1)S(1)}, u32[]{:S(2)}, u32[]{:S(2)}) async-start(bf16[64,8,128]{2,1,0:T(8,128)(2,1)} %collective-permute-done.16), calls=%async_computation | async-start | bytes 262144 | tf_op jit(solution)/shard_map/all_to_all | solution.py:333
  106.3 2.5 %shard_map.97.index_ref = s32[256]{0:T(256)S(1)} custom-call(s32[8,64]{1,0:T(8,128)S(1)} %copy-done.7), custom_call_target="tpu_custom_call" | custom-call | bytes 256 | tf_op jit(solution)/shard_map/pallas_call | solution.py:319
  108.8 12.1 %all-to-all-done.pieces_ref = bf16[64,8,128]{2,1,0:T(8,128)(2,1)S(1)} async-done(((bf16[64,8,128]{2,1,0:T(8,128)(2,1)}), bf16[64,8,128]{2,1,0:T(8,128)(2,1)S(1)}, u32[]{:S(2)}, u32[]{:S(2)}) %all-to-all-start) | async-done | bytes 131104 | tf_op jit(solution)/shard_map/all_to_all | solution.py:333
  120.9 1.6 %shard_map.98 = bf16[64,4,8,128]{3,2,1,0:T(8,128)(2,1)} custom-call(s32[256]{0:T(256)S(1)} %shard_map.97.index_ref, bf16[64,8,128]{2,1,0:T(8,128)(2,1)S(1)} %all-to-all-done.pieces_ref), custom_call_target="tpu_custom_call" | custom-call | bytes 1048576 | tf_op jit(solution)/shard_map/pallas_call | solution.py:334
  122.6 5.8 %all-to-all-start.1 = ((bf16[64,4,8,128]{3,2,1,0:T(8,128)(2,1)}), bf16[64,4,8,128]{3,2,1,0:T(8,128)(2,1)S(1)}, u32[]{:S(2)}, u32[]{:S(2)}) async-start(bf16[64,4,8,128]{3,2,1,0:T(8,128)(2,1)} %shard_map.98), calls=%async_computation.1 | async-start | bytes 1048576 | tf_op jit(solution)/shard_map/all_to_all | solution.py:341
  128.3 1.8 %shard_map.96 = f32[1024,256]{1,0:T(8,128)} custom-call(s32[8]{0:T(128)S(1)} %bitcast.43, s32[2,8]{1,0:T(2,128)S(1)} %bitcast.54, bf16[256,512]{1,0:T(8,128)(2,1)S(1)} %get-tuple-element.112.residual_ref, bf16[256,256]{1,0:T(8,128)(2,1)S(1)} %get-tuple-element.113.item_ref, f32[1024,256]{1,0:T(8,128)S(1)} %get-tuple-element.114.user_ref), custom_call_target="tpu_custom_call" | custom-call | flops 67108864 | bytes 1048576 | tf_op jit(solution)/shard_map/pallas_call | solution.py:304
  130.1 28.3 %all-to-all-done.1 = bf16[64,4,8,128]{3,2,1,0:T(8,128)(2,1)S(1)} async-done(((bf16[64,4,8,128]{3,2,1,0:T(8,128)(2,1)}), bf16[64,4,8,128]{3,2,1,0:T(8,128)(2,1)S(1)}, u32[]{:S(2)}, u32[]{:S(2)}) %all-to-all-start.1) | async-done | bytes 524320 | tf_op jit(solution)/shard_map/all_to_all | solution.py:341
  (53 shorter events, 25.7 us)
Async XLA Ops:
  0.6 7.4 %copy-start.3 = (s32[1,1,8]{2,1,0:T(1,128)S(1)}, s32[1,1,8]{2,1,0:T(1,128)}, u32[]{:S(2)}) copy-start(s32[1,1,8]{2,1,0:T(1,128)} %param.10) | copy-start | bytes 100
  0.6 7.4 %copy-start.6 = (s32[1,1,8,2]{2,3,1,0:T(2,128)S(1)}, s32[1,1,8,2]{2,3,1,0:T(2,128)}, u32[]{:S(2)}) copy-start(s32[1,1,8,2]{2,3,1,0:T(2,128)} %param.9) | copy-start | bytes 196
  0.7 7.4 %copy-start = (bf16[1,1,8,2,256,256]{5,4,3,2,1,0:T(8,128)(2,1)S(1)}, bf16[1,1,8,2,256,256]{5,4,3,2,1,0:T(8,128)(2,1)}, u32[]{:S(2)}) copy-start(bf16[1,1,8,2,256,256]{5,4,3,2,1,0:T(8,128)(2,1)} %param.8) | copy-start | bytes 6291460
  0.7 7.4 %copy-start.1 = (f32[1,1024,256]{2,1,0:T(8,128)S(1)}, f32[1,1024,256]{2,1,0:T(8,128)}, u32[]{:S(2)}) copy-start(f32[1,1024,256]{2,1,0:T(8,128)} %param.6) | copy-start | bytes 3145732
  3.6 9.1 %collective-permute-start = (bf16[256,256]{1,0:T(8,128)(2,1)}, bf16[256,256]{1,0:T(8,128)(2,1)S(1)}, u32[]{:S(2)}, u32[]{:S(2)}) collective-permute-start(bf16[256,256]{1,0:T(8,128)(2,1)} %get-tuple-element.59.refs_1_), channel_id=1, source_target_pairs={{0,8},{8,16},{16,24},{24,32},{32,40},{40,48},{48,56},{64,72},{72,8... | collective-permute-start | bytes 393224 | tf_op jit(solution)/shard_map/ppermute | solution.py:295
  13.7 3.8 %collective-permute-start.1 = (bf16[256,256]{1,0:T(8,128)(2,1)S(1)}, bf16[256,256]{1,0:T(8,128)(2,1)S(1)}, u32[]{:S(2)}, u32[]{:S(2)}) collective-permute-start(bf16[256,256]{1,0:T(8,128)(2,1)S(1)} %get-tuple-element.64.refs_1_), channel_id=1, source_target_pairs={{8,16},{16,24},{24,32},{32,40},{40,48},{48,56},{72,80},{80,88},{88... | collective-permute-start | bytes 393224 | tf_op jit(solution)/shard_map/ppermute | solution.py:295
  15.6 4.6 %collective-permute-start.3 = (bf16[256,256]{1,0:T(8,128)(2,1)S(1)}, bf16[256,256]{1,0:T(8,128)(2,1)S(1)}, u32[]{:S(2)}, u32[]{:S(2)}) collective-permute-start(bf16[256,256]{1,0:T(8,128)(2,1)S(1)} %copy-done.5), channel_id=1, source_target_pairs={{56,64},{120,128},{184,192},{248,256},{312,320},{376,384},{440,448... | collective-permute-start | bytes 393224 | tf_op jit(solution)/shard_map/ppermute | solution.py:297
  18.1 2.1 %collective-permute-start.2 = (bf16[256,256]{1,0:T(8,128)(2,1)S(1)}, bf16[256,256]{1,0:T(8,128)(2,1)S(1)}, u32[]{:S(2)}, u32[]{:S(2)}) collective-permute-start(bf16[256,256]{1,0:T(8,128)(2,1)S(1)} %get-tuple-element.70.refs_1_), channel_id=1, source_target_pairs={{16,24},{24,32},{32,40},{40,48},{48,56},{80,88},{88,96},{96,104},{... | collective-permute-start | bytes 393224 | tf_op jit(solution)/shard_map/ppermute | solution.py:295
  18.7 5.0 %collective-permute-start.5 = (bf16[256,256]{1,0:T(8,128)(2,1)S(1)}, bf16[256,256]{1,0:T(8,128)(2,1)S(1)}, u32[]{:S(2)}, u32[]{:S(2)}) collective-permute-start(bf16[256,256]{1,0:T(8,128)(2,1)S(1)} %get-tuple-element.64.refs_1_), channel_id=1, source_target_pairs={{56,64},{120,128},{184,192},{248,256},{312,320},{376,384},{440,448... | collective-permute-start | bytes 393224 | tf_op jit(solution)/shard_map/ppermute | solution.py:297
  20.8 13.1 %collective-permute-start.4 = (bf16[256,256]{1,0:T(8,128)(2,1)S(1)}, bf16[256,256]{1,0:T(8,128)(2,1)S(1)}, u32[]{:S(2)}, u32[]{:S(2)}) collective-permute-start(bf16[256,256]{1,0:T(8,128)(2,1)S(1)} %get-tuple-element.76.refs_1_), channel_id=1, source_target_pairs={{0,8},{24,32},{32,40},{40,48},{48,56},{64,72},{88,96},{96,104},{10... | collective-permute-start | bytes 393224 | tf_op jit(solution)/shard_map/ppermute | solution.py:295
  22.1 17.0 %collective-permute-start.7 = (bf16[256,256]{1,0:T(8,128)(2,1)S(1)}, bf16[256,256]{1,0:T(8,128)(2,1)S(1)}, u32[]{:S(2)}, u32[]{:S(2)}) collective-permute-start(bf16[256,256]{1,0:T(8,128)(2,1)S(1)} %get-tuple-element.70.refs_1_), channel_id=1, source_target_pairs={{56,64},{120,128},{184,192},{248,256},{312,320},{376,384},{440,448... | collective-permute-start | bytes 393224 | tf_op jit(solution)/shard_map/ppermute | solution.py:297
  35.0 4.1 %collective-permute-start.6 = (bf16[256,256]{1,0:T(8,128)(2,1)S(1)}, bf16[256,256]{1,0:T(8,128)(2,1)S(1)}, u32[]{:S(2)}, u32[]{:S(2)}) collective-permute-start(bf16[256,256]{1,0:T(8,128)(2,1)S(1)} %get-tuple-element.82.refs_1_), channel_id=1, source_target_pairs={{0,8},{8,16},{32,40},{40,48},{48,56},{64,72},{72,80},{96,104},{104... | collective-permute-start | bytes 393224 | tf_op jit(solution)/shard_map/ppermute | solution.py:295
  36.9 9.5 %collective-permute-start.9 = (bf16[256,256]{1,0:T(8,128)(2,1)S(1)}, bf16[256,256]{1,0:T(8,128)(2,1)S(1)}, u32[]{:S(2)}, u32[]{:S(2)}) collective-permute-start(bf16[256,256]{1,0:T(8,128)(2,1)S(1)} %get-tuple-element.76.refs_1_), channel_id=1, source_target_pairs={{56,64},{120,128},{184,192},{248,256},{312,320},{376,384},{440,448... | collective-permute-start | bytes 393224 | tf_op jit(solution)/shard_map/ppermute | solution.py:297
  40.1 11.2 %collective-permute-start.8 = (bf16[256,256]{1,0:T(8,128)(2,1)S(1)}, bf16[256,256]{1,0:T(8,128)(2,1)S(1)}, u32[]{:S(2)}, u32[]{:S(2)}) collective-permute-start(bf16[256,256]{1,0:T(8,128)(2,1)S(1)} %get-tuple-element.88.refs_1_), channel_id=1, source_target_pairs={{0,8},{8,16},{16,24},{40,48},{48,56},{64,72},{72,80},{80,88},{104,... | collective-permute-start | bytes 393224 | tf_op jit(solution)/shard_map/ppermute | solution.py:295
  44.3 12.1 %collective-permute-start.11 = (bf16[256,256]{1,0:T(8,128)(2,1)S(1)}, bf16[256,256]{1,0:T(8,128)(2,1)S(1)}, u32[]{:S(2)}, u32[]{:S(2)}) collective-permute-start(bf16[256,256]{1,0:T(8,128)(2,1)S(1)} %get-tuple-element.82.refs_1_), channel_id=1, source_target_pairs={{56,64},{120,128},{184,192},{248,256},{312,320},{376,384},{440,448... | collective-permute-start | bytes 393224 | tf_op jit(solution)/shard_map/ppermute | solution.py:297
  52.3 4.1 %collective-permute-start.10 = (bf16[256,256]{1,0:T(8,128)(2,1)S(1)}, bf16[256,256]{1,0:T(8,128)(2,1)S(1)}, u32[]{:S(2)}, u32[]{:S(2)}) collective-permute-start(bf16[256,256]{1,0:T(8,128)(2,1)S(1)} %get-tuple-element.94.refs_1_), channel_id=1, source_target_pairs={{0,8},{8,16},{16,24},{24,32},{48,56},{64,72},{72,80},{80,88},{88,9... | collective-permute-start | bytes 393224 | tf_op jit(solution)/shard_map/ppermute | solution.py:295
  54.3 9.4 %collective-permute-start.13 = (bf16[256,256]{1,0:T(8,128)(2,1)S(1)}, bf16[256,256]{1,0:T(8,128)(2,1)S(1)}, u32[]{:S(2)}, u32[]{:S(2)}) collective-permute-start(bf16[256,256]{1,0:T(8,128)(2,1)S(1)} %get-tuple-element.88.refs_1_), channel_id=1, source_target_pairs={{56,64},{120,128},{184,192},{248,256},{312,320},{376,384},{440,448... | collective-permute-start | bytes 393224 | tf_op jit(solution)/shard_map/ppermute | solution.py:297
  57.5 11.2 %collective-permute-start.12 = (bf16[256,256]{1,0:T(8,128)(2,1)S(1)}, bf16[256,256]{1,0:T(8,128)(2,1)S(1)}, u32[]{:S(2)}, u32[]{:S(2)}) collective-permute-start(bf16[256,256]{1,0:T(8,128)(2,1)S(1)} %get-tuple-element.100.refs_1_), channel_id=1, source_target_pairs={{0,8},{8,16},{16,24},{24,32},{32,40},{64,72},{72,80},{80,88},{88,9... | collective-permute-start | bytes 393224 | tf_op jit(solution)/shard_map/ppermute | solution.py:295
  61.6 11.2 %collective-permute-start.15 = (bf16[256,256]{1,0:T(8,128)(2,1)S(1)}, bf16[256,256]{1,0:T(8,128)(2,1)S(1)}, u32[]{:S(2)}, u32[]{:S(2)}) collective-permute-start(bf16[256,256]{1,0:T(8,128)(2,1)S(1)} %get-tuple-element.94.refs_1_), channel_id=1, source_target_pairs={{56,64},{120,128},{184,192},{248,256},{312,320},{376,384},{440,448... | collective-permute-start | bytes 393224 | tf_op jit(solution)/shard_map/ppermute | solution.py:297
  69.7 4.1 %collective-permute-start.14 = (bf16[256,256]{1,0:T(8,128)(2,1)S(1)}, bf16[256,256]{1,0:T(8,128)(2,1)S(1)}, u32[]{:S(2)}, u32[]{:S(2)}) collective-permute-start(bf16[256,256]{1,0:T(8,128)(2,1)S(1)} %get-tuple-element.106.refs_1_), channel_id=1, source_target_pairs={{0,8},{8,16},{16,24},{24,32},{32,40},{40,48},{64,72},{72,80},{80,8... | collective-permute-start | bytes 393224 | tf_op jit(solution)/shard_map/ppermute | solution.py:295
  71.7 34.6 %copy-start.7 = (s32[8,64]{1,0:T(8,128)S(1)}, s32[8,64]{1,0:T(8,128)}, u32[]{:S(2)}) copy-start(s32[8,64]{1,0:T(8,128)} %plan_ref.1) | copy-start | bytes 6148
  74.9 11.8 %collective-permute-start.16 = (bf16[64,8,128]{2,1,0:T(8,128)(2,1)S(1)}, bf16[64,8,128]{2,1,0:T(8,128)(2,1)}, u32[]{:S(2)}, u32[]{:S(2)}) collective-permute-start(bf16[64,8,128]{2,1,0:T(8,128)(2,1)S(1)} %bitcast.55), channel_id=1, source_target_pairs={{0,1},{1,2},{2,3},{3,452},{4,5},{5,6},{6,7},{7,448},{8,9},{9,10},{... | collective-permute-start | bytes 393224 | tf_op jit(solution)/shard_map/ppermute | solution.py:332
  86.6 34.3 %all-to-all-start = ((bf16[64,8,128]{2,1,0:T(8,128)(2,1)}), bf16[64,8,128]{2,1,0:T(8,128)(2,1)S(1)}, u32[]{:S(2)}, u32[]{:S(2)}) async-start(bf16[64,8,128]{2,1,0:T(8,128)(2,1)} %collective-permute-done.16), calls=%async_computation | async-start | bytes 262144 | tf_op jit(solution)/shard_map/all_to_all | solution.py:333
  122.6 35.9 %all-to-all-start.1 = ((bf16[64,4,8,128]{3,2,1,0:T(8,128)(2,1)}), bf16[64,4,8,128]{3,2,1,0:T(8,128)(2,1)S(1)}, u32[]{:S(2)}, u32[]{:S(2)}) async-start(bf16[64,4,8,128]{3,2,1,0:T(8,128)(2,1)} %shard_map.98), calls=%async_computation.1 | async-start | bytes 1048576 | tf_op jit(solution)/shard_map/all_to_all | solution.py:341
  (3 other events, 4.6 us)

commit v3 on v2

--- a/solution.py
+++ b/solution.py
@@ -56,15 +56,13 @@
     return slot - LAG if inner + LAG < slot < stops + LAG else None
 
 
-def plan_slot(slot, stops, count_ref):
+def plan_slot(slot, stops):
     inner = lax.rem(lax.axis_index("blk"), PLANE)
     early = jnp.logical_and(slot <= inner, slot < stops)
     late = jnp.logical_and(slot > inner + LAG, slot < stops + LAG)
     active = jnp.logical_or(early, late)
     stop = jnp.clip(jnp.where(late, slot - LAG, slot), 0, stops - 1)
-    count = jnp.where(active, count_ref[stop], 0)
-    crossed = jnp.logical_and(late, inner == 0)
-    return active, stop, count, crossed
+    return active, stop, jnp.logical_and(late, inner == 0), lax.rem(inner, 2)
 
 
 def fetch(stop, count, row_ref, user_ref, low_ref, rated_ref, tiles, copy):
@@ -91,7 +89,7 @@
             rated_ref[:, rows] = tiles[c].T
 
 
-def update_items(exact, item_low, count, low_ref, rated_ref, residual_ref, item_ref):
+def update_items(exact, item_low, decay, low_ref, rated_ref, residual_ref, item_ref):
     item_ref[...] = item_low
     tile = item_ref.shape[0]
     grad = None
@@ -105,7 +103,6 @@
         residual_ref[:, span] = residual
         part = jnp.dot(residual, low, preferred_element_type=F32)
         grad = part if grad is None else grad + part
-    decay = shrinkage * count.astype(F32)
     return (exact + learn_rate * (grad - decay * exact)).astype(BF16)
 
 
@@ -130,14 +127,17 @@
     moves[3].wait()
     exact = exact_ref[...]
     next_ref[...] = update_items(
-        exact, exact.astype(BF16), count, low_ref, rated_ref, residual_ref, item_ref
+        exact, exact.astype(BF16), shrinkage * count.astype(F32), low_ref, rated_ref,
+        residual_ref, item_ref,
     )
 
 
-def item_body(slot, stops, last, n_in, count_ref, *refs):
-    sources = refs[:n_in]
-    low_ref, rated_ref, next_ref, residual_ref, item_ref = refs[n_in:]
-    active, _, count, crossed = plan_slot(slot, stops, count_ref)
+def item_body(slot, stops, parity, last, arrivals, *refs):
+    sources = refs[:arrivals]
+    held_ref, low_ref, rated_ref, decay_ref = refs[arrivals : arrivals + 4]
+    others = refs[arrivals + 4 : -3]
+    next_ref, residual_ref, item_ref = refs[-3:]
+    active, _, crossed, own = plan_slot(slot, stops)
 
     def emit(block):
         if last:
@@ -148,26 +148,41 @@
         else:
             next_ref[...] = block
 
-    @pl.when(active)
+    @pl.when(jnp.logical_and(own == parity, active))
     def _():
         item_low = sources[0][...]
-        if n_in == 3:
-            item_low = jnp.where(crossed, sources[2][...], item_low)
-        exact = item_low.astype(F32)
-        emit(update_items(exact, item_low, count, low_ref, rated_ref, residual_ref, item_ref))
-
-    @pl.when(jnp.logical_not(active))
+        if arrivals == 2:
+            item_low = jnp.where(crossed, sources[1][...], item_low)
+        emit(
+            update_items(
+                item_low.astype(F32), item_low, decay_ref[0:1, :], low_ref, rated_ref,
+                residual_ref, item_ref,
+            )
+        )
+
+    @pl.when(jnp.logical_and(own == parity, jnp.logical_not(active)))
     def _():
-        emit(sources[1][...])
+        emit(held_ref[...])
+
+    if others:
+
+        @pl.when(own != parity)
+        def _():
+            emit(others[0][...])
+            residual_ref[...] = others[1][...]
+            item_ref[...] = others[2][...]
 
 
 def user_body(slot, stops, last, count_ref, row_ref, residual_ref, item_ref, user_ref, *refs):
-    _, stop, count, _ = plan_slot(slot, stops, count_ref)
+    active, stop, _, _ = plan_slot(slot, stops)
+    count = jnp.where(active, count_ref[stop], 0)
     if last:
         (out_ref,) = refs
     else:
-        ratings_ref, out_ref, low_ref, rated_ref, tiles, sem = refs
-        next_active, next_stop, next_count, _ = plan_slot(slot + 1, stops, count_ref)
+        ratings_ref, out_ref, low_ref, rated_ref, decay_ref, tiles, sem = refs
+        next_active, next_stop, _, _ = plan_slot(slot + 1, stops)
+        next_count = jnp.where(next_active, count_ref[next_stop], 0)
+        decay_ref[...] = jnp.full(decay_ref.shape, shrinkage * next_count.astype(F32))
         copy = pltpu.make_async_copy(ratings_ref.at[next_stop], tiles, sem)
         pl.when(next_active)(copy.start)
     tile = item_ref.shape[0]
@@ -249,6 +264,7 @@
     low_shape = jax.ShapeDtypeStruct((wide, rank), BF16)
     rated_shape = jax.ShapeDtypeStruct((items, wide), BF16)
     block_shape = jax.ShapeDtypeStruct((items, rank), BF16)
+    decay_shape = jax.ShapeDtypeStruct((8, rank), F32)
     piece_shape = jax.ShapeDtypeStruct((items // 8, rank // 128, 8, 128), BF16)
     user_shape = jax.ShapeDtypeStruct(users.shape, F32)
     tile_scratch = [pltpu.VMEM((tiles_at_stop, tile, tile), BF16), pltpu.SemaphoreType.DMA]
@@ -272,31 +288,46 @@
     )(count_table, row_table, users, item_factors[0], rating_tiles)
 
     across = [(b, (b + 1) % blocks) for b in range(PLANE - 1, blocks, PLANE)]
+
+    def within(slot, parity):
+        pairs = []
+        for b in range(blocks):
+            inner = b % PLANE
+            if inner % 2 == parity and inner != PLANE - 1:
+                here, there = stop_at(slot, inner, stops), stop_at(slot + 1, inner + 1, stops)
+                if here is not None and there == here + 1:
+                    pairs.append((b, b + 1))
+        return pairs
+
+    odd_block = block
+    from_odd = from_even = None
     crossing = {}
     for slot in range(slots):
         last = slot == slots - 1
-        if slot > 0:
-            block, residual, item_low = call(
-                functools.partial(item_body, slot, stops, last, len(arrived)),
-                (piece_shape if last else block_shape, rated_shape, block_shape),
-                [SMEM] + [VMEM] * (len(arrived) + 2),
+
+        def items_call(parity, arrived, others):
+            ends = last and parity == 0
+            return call(
+                functools.partial(item_body, slot, stops, parity, ends, len(arrived)),
+                (piece_shape if ends else block_shape, rated_shape, block_shape),
+                [VMEM] * (len(arrived) + 4 + len(others)),
                 (VMEM, VMEM, VMEM),
                 (),
-                4 * items * wide * rank,
-            )(count_table, *arrived, low, rated)
+                2 * items * wide * rank,
+            )(*arrived, block, low, rated, decay, *others)
+
+        if slot > 0:
+            others = items_call(1, [from_even], ())
+            odd_block = others[0]
+        arrived = [from_odd] + ([crossing[slot]] if slot in crossing else [])
         if not last:
-            within = [
-                (b, b + 1)
-                for b in range(blocks)
-                if b % PLANE != PLANE - 1
-                and stop_at(slot, b % PLANE, stops) is not None
-                and stop_at(slot + 1, b % PLANE + 1, stops) == stop_at(slot, b % PLANE, stops) + 1
-            ]
-            arrived = [lax.ppermute(block, "blk", within), block]
-            if slot < stops - 1:
-                crossing[slot + 1 + LAG] = lax.ppermute(block, "blk", across)
-            if slot + 1 in crossing:
-                arrived.append(crossing[slot + 1])
+            from_odd = lax.ppermute(odd_block, "blk", within(slot, 1))
+        if slot < stops - 1:
+            crossing[slot + 1 + LAG] = lax.ppermute(odd_block, "blk", across)
+        if slot > 0:
+            block, residual, item_low = items_call(0, arrived, others)
+        if not last:
+            from_even = lax.ppermute(block, "blk", within(slot, 0))
         body = functools.partial(user_body, slot, stops, last)
         operands = (count_table, row_table, residual, item_low, users)
         flops = 2 * wide * items * rank
@@ -305,11 +336,11 @@
                 body, user_shape, [SMEM, SMEM, VMEM, VMEM, VMEM], VMEM, (), flops
             )(*operands)
         else:
-            users, low, rated = call(
+            users, low, rated, decay = call(
                 body,
-                (user_shape, low_shape, rated_shape),
+                (user_shape, low_shape, rated_shape, decay_shape),
                 [SMEM, SMEM, VMEM, VMEM, VMEM, ANY],
-                (VMEM, VMEM, VMEM),
+                (VMEM, VMEM, VMEM, VMEM),
                 tile_scratch,
                 flops,
                 alias={4: 0} if slot else {},

time: 160 us -> 210 us (1.31)
  waiting for transfers between devices: 72.5 us -> 116 us
  starting transfers between devices: 54.9 us -> 65.8 us
  Pallas kernels: 29 us -> 24.7 us
    ppermute x16 -> x25, waiting for transfers between devices: 22.9 us -> 69.4 us  [the longest x9 68.4 us: shards(): from_even = lax.ppermute(block, 'blk', within(slot, 0))]
    ppermute x16 -> x25, starting transfers between devices: 26.9 us -> 32.4 us  [the longest x9 17.2 us: shards(): from_odd = lax.ppermute(odd_block, 'blk', within(slot, 1))]
    all_to_all x1, starting transfers between devices: 19.7 us -> 24.5 us  [shards(): lax.all_to_all(shifted, 'blk', split_axis=0, concat_axis=0, tiled=True)]
    pallas_call x18 -> x27, Pallas kernels: 19.3 us -> 14.9 us  [the longest x9 10.7 us: shards(): call(body, (user_shape, low_shape, rated_shape, decay_shape), [SMEM, SMEM...]
    ppermute x1, waiting for transfers between devices: 9.22 us -> 5.92 us  [shards(): shifted = lax.ppermute(pieces, ('blk', 'group'), moves)]
  transfers between devices with their start and end apart: 19 -> 28, of which waited for: 9 -> 10; matrix products, arithmetic and copies ran while one was open for 0% -> 0% of each run, Pallas kernels for 13% -> 9%
where the time goes in v3:
time: 210 us; the launch traced here: 209 us
  waiting for transfers between devices  116 us (55%)
  starting transfers between devices  65.8 us (31%)
  Pallas kernels  24.7 us (12%)
    ppermute x9, waiting for transfers between devices, shards(): from_even = lax.ppermute(block, 'blk', within(slot, 0))  68.4 us
    all_to_all x1, waiting for transfers between devices, shards(): lax.all_to_all(picked, 'blk', split_axis=0, concat_axis=0, tiled=True)  28.3 us
    all_to_all x1, starting transfers between devices, shards(): lax.all_to_all(shifted, 'blk', split_axis=0, concat_axis=0, tiled=True)  24.5 us
    ppermute x9, starting transfers between devices, shards(): from_odd = lax.ppermute(odd_block, 'blk', within(slot, 1))  17.2 us
    all_to_all x1, waiting for transfers between devices, shards(): lax.all_to_all(shifted, 'blk', split_axis=0, concat_axis=0, tiled=True)  12.1 us
    pallas_call x9, Pallas kernels, shards(): call(body, (user_shape, low_shape, rated_shape, decay_shape), [SMEM, SMEM...  10.7 us
    ppermute x9, starting transfers between devices, shards(): from_even = lax.ppermute(block, 'blk', within(slot, 0))  10.5 us
    ppermute x1, waiting for transfers between devices, shards(): shifted = lax.ppermute(pieces, ('blk', 'group'), moves)  5.92 us
  transfers between devices with their start and end apart: 28, of which 10 were waited for; matrix products, arithmetic and copies ran while one was open for 0% of the time, Pallas kernels for 9%

profile of v3, /device:TPU:1, one launch (start us, length us, event | category | flops | bytes accessed | tf_op | source)
XLA Modules:
  0.0 209.4 jit_solution(10543739337757690498)
XLA Ops:
  0.7 2.9 %shard_map.77 = (bf16[256,256]{1,0:T(8,128)(2,1)}, bf16[256,512]{1,0:T(8,128)(2,1)}, bf16[256,256]{1,0:T(8,128)(2,1)}) custom-call(s32[8]{0:T(128)} %bitcast.35, s32[2,8]{1,0:T(2,128)} %bitcast.24, f32[1024,256]{1,0:T(8,128)} %bitcast.21, f32[256,256]{1,0:T(8,128)} %bitcast.49, bf16[8,2,256,256]{3,2,1,0:T(8,128)(2,1)} %bitcast.11), custom_call_target="tpu_custom_call" | custom-call | flops 134217728 | bytes 1048576 | tf_op jit(solution)/shard_map/pallas_call | solution.py:271
  3.6 1.4 collective-permute-start.1
  5.0 4.8 %collective-permute-start = (bf16[256,256]{1,0:T(8,128)(2,1)}, bf16[256,256]{1,0:T(8,128)(2,1)S(1)}, u32[]{:S(2)}, u32[]{:S(2)}) collective-permute-start(bf16[256,256]{1,0:T(8,128)(2,1)} %get-tuple-element.95.refs_1_), channel_id=1, source_target_pairs={{8,16},{24,32},{40,48},{72,80},{88,96},{104,112},{136,144},{152,16... | collective-permute-start | bytes 393224 | tf_op jit(solution)/shard_map/ppermute | solution.py:324
  14.3 4.6 %collective-permute-start.5 = (bf16[256,256]{1,0:T(8,128)(2,1)S(1)}, bf16[256,256]{1,0:T(8,128)(2,1)S(1)}, u32[]{:S(2)}, u32[]{:S(2)}) collective-permute-start(bf16[256,256]{1,0:T(8,128)(2,1)S(1)} %get-tuple-element.101.refs_5_), channel_id=1, source_target_pairs={{8,16},{24,32},{40,48},{72,80},{88,96},{104,112},{136,144},{152,16... | collective-permute-start | bytes 393224 | tf_op jit(solution)/shard_map/ppermute | solution.py:324
  27.4 10.6 %collective-permute-done.7.refs_0_ = bf16[256,256]{1,0:T(8,128)(2,1)S(1)} collective-permute-done((bf16[256,256]{1,0:T(8,128)(2,1)S(1)}, bf16[256,256]{1,0:T(8,128)(2,1)S(1)}, u32[]{:S(2)}, u32[]{:S(2)}) %collective-permute-start.7) | collective-permute-done | bytes 131104 | tf_op jit(solution)/shard_map/ppermute | solution.py:330
  41.8 1.4 shard_map.90
  43.3 11.5 %collective-permute-done.12.refs_0_ = bf16[256,256]{1,0:T(8,128)(2,1)S(1)} collective-permute-done((bf16[256,256]{1,0:T(8,128)(2,1)S(1)}, bf16[256,256]{1,0:T(8,128)(2,1)S(1)}, u32[]{:S(2)}, u32[]{:S(2)}) %collective-permute-start.12) | collective-permute-done | bytes 131104 | tf_op jit(solution)/shard_map/ppermute | solution.py:330
  58.7 1.4 shard_map.93
  60.1 11.5 %collective-permute-done.13.refs_0_ = bf16[256,256]{1,0:T(8,128)(2,1)S(1)} collective-permute-done((bf16[256,256]{1,0:T(8,128)(2,1)S(1)}, bf16[256,256]{1,0:T(8,128)(2,1)S(1)}, u32[]{:S(2)}, u32[]{:S(2)}) %collective-permute-start.13) | collective-permute-done | bytes 131104 | tf_op jit(solution)/shard_map/ppermute | solution.py:330
  74.2 1.3 collective-permute-start.14
  75.5 1.4 shard_map.96
  77.0 11.5 %collective-permute-done.18.refs_0_ = bf16[256,256]{1,0:T(8,128)(2,1)S(1)} collective-permute-done((bf16[256,256]{1,0:T(8,128)(2,1)S(1)}, bf16[256,256]{1,0:T(8,128)(2,1)S(1)}, u32[]{:S(2)}, u32[]{:S(2)}) %collective-permute-start.18) | collective-permute-done | bytes 131104 | tf_op jit(solution)/shard_map/ppermute | solution.py:330
  92.3 1.3 shard_map.99
  93.7 11.6 %collective-permute-done.19.refs_0_ = bf16[256,256]{1,0:T(8,128)(2,1)S(1)} collective-permute-done((bf16[256,256]{1,0:T(8,128)(2,1)S(1)}, bf16[256,256]{1,0:T(8,128)(2,1)S(1)}, u32[]{:S(2)}, u32[]{:S(2)}) %collective-permute-start.19) | collective-permute-done | bytes 131104 | tf_op jit(solution)/shard_map/ppermute | solution.py:330
  110.3 11.8 %collective-permute-done.24.refs_0_ = bf16[256,256]{1,0:T(8,128)(2,1)S(1)} collective-permute-done((bf16[256,256]{1,0:T(8,128)(2,1)S(1)}, bf16[256,256]{1,0:T(8,128)(2,1)S(1)}, u32[]{:S(2)}, u32[]{:S(2)}) %collective-permute-start.24) | collective-permute-done | bytes 131104 | tf_op jit(solution)/shard_map/ppermute | solution.py:330
  122.7 3.2 %collective-permute-start.25 = (bf16[64,8,128]{2,1,0:T(8,128)(2,1)S(1)}, bf16[64,8,128]{2,1,0:T(8,128)(2,1)}, u32[]{:S(2)}, u32[]{:S(2)}) collective-permute-start(bf16[64,8,128]{2,1,0:T(8,128)(2,1)S(1)} %bitcast.46), channel_id=1, source_target_pairs={{0,1},{1,2},{2,3},{3,452},{4,5},{5,6},{6,7},{7,448},{8,9},{9,10},{... | collective-permute-start | bytes 393224 | tf_op jit(solution)/shard_map/ppermute | solution.py:363
  126.0 5.9 %collective-permute-done.25 = bf16[64,8,128]{2,1,0:T(8,128)(2,1)} collective-permute-done((bf16[64,8,128]{2,1,0:T(8,128)(2,1)S(1)}, bf16[64,8,128]{2,1,0:T(8,128)(2,1)}, u32[]{:S(2)}, u32[]{:S(2)}) %collective-permute-start.25) | collective-permute-done | bytes 131104 | tf_op jit(solution)/shard_map/ppermute | solution.py:363
  131.9 24.5 %all-to-all-start = ((bf16[64,8,128]{2,1,0:T(8,128)(2,1)}), bf16[64,8,128]{2,1,0:T(8,128)(2,1)S(1)}, u32[]{:S(2)}, u32[]{:S(2)}) async-start(bf16[64,8,128]{2,1,0:T(8,128)(2,1)} %collective-permute-done.25), calls=%async_computation | async-start | bytes 262144 | tf_op jit(solution)/shard_map/all_to_all | solution.py:364
  156.4 2.5 %shard_map.106.index_ref = s32[256]{0:T(256)S(1)} custom-call(s32[8,64]{1,0:T(8,128)S(1)} %copy-done.7), custom_call_target="tpu_custom_call" | custom-call | bytes 256 | tf_op jit(solution)/shard_map/pallas_call | solution.py:350
  158.9 12.1 %all-to-all-done.pieces_ref = bf16[64,8,128]{2,1,0:T(8,128)(2,1)S(1)} async-done(((bf16[64,8,128]{2,1,0:T(8,128)(2,1)}), bf16[64,8,128]{2,1,0:T(8,128)(2,1)S(1)}, u32[]{:S(2)}, u32[]{:S(2)}) %all-to-all-start) | async-done | bytes 131104 | tf_op jit(solution)/shard_map/all_to_all | solution.py:364
  171.0 1.6 shard_map.107
  172.6 5.8 %all-to-all-start.1 = ((bf16[64,4,8,128]{3,2,1,0:T(8,128)(2,1)}), bf16[64,4,8,128]{3,2,1,0:T(8,128)(2,1)S(1)}, u32[]{:S(2)}, u32[]{:S(2)}) async-start(bf16[64,4,8,128]{3,2,1,0:T(8,128)(2,1)} %shard_map.107), calls=%async_computation.1 | async-start | bytes 1048576 | tf_op jit(solution)/shard_map/all_to_all | solution.py:372
  178.4 1.8 shard_map.105
  180.2 28.3 %all-to-all-done.1 = bf16[64,4,8,128]{3,2,1,0:T(8,128)(2,1)S(1)} async-done(((bf16[64,4,8,128]{3,2,1,0:T(8,128)(2,1)}), bf16[64,4,8,128]{3,2,1,0:T(8,128)(2,1)S(1)}, u32[]{:S(2)}, u32[]{:S(2)}) %all-to-all-start.1) | async-done | bytes 524320 | tf_op jit(solution)/shard_map/all_to_all | solution.py:372
  (80 shorter events, 33.3 us)
Async XLA Ops:
  3.6 9.4 %collective-permute-start.1 = (bf16[256,256]{1,0:T(8,128)(2,1)}, bf16[256,256]{1,0:T(8,128)(2,1)S(1)}, u32[]{:S(2)}, u32[]{:S(2)}) collective-permute-start(bf16[256,256]{1,0:T(8,128)(2,1)} %get-tuple-element.95.refs_1_), channel_id=1, source_target_pairs={{0,8},{16,24},{32,40},{48,56},{64,72},{80,88},{96,104},{112,120},{... | collective-permute-start | bytes 393224 | tf_op jit(solution)/shard_map/ppermute | solution.py:330
  5.0 8.5 %collective-permute-start = (bf16[256,256]{1,0:T(8,128)(2,1)}, bf16[256,256]{1,0:T(8,128)(2,1)S(1)}, u32[]{:S(2)}, u32[]{:S(2)}) collective-permute-start(bf16[256,256]{1,0:T(8,128)(2,1)} %get-tuple-element.95.refs_1_), channel_id=1, source_target_pairs={{8,16},{24,32},{40,48},{72,80},{88,96},{104,112},{136,144},{152,16... | collective-permute-start | bytes 393224 | tf_op jit(solution)/shard_map/ppermute | solution.py:324
  14.3 6.5 %collective-permute-start.5 = (bf16[256,256]{1,0:T(8,128)(2,1)S(1)}, bf16[256,256]{1,0:T(8,128)(2,1)S(1)}, u32[]{:S(2)}, u32[]{:S(2)}) collective-permute-start(bf16[256,256]{1,0:T(8,128)(2,1)S(1)} %get-tuple-element.101.refs_5_), channel_id=1, source_target_pairs={{8,16},{24,32},{40,48},{72,80},{88,96},{104,112},{136,144},{152,16... | collective-permute-start | bytes 393224 | tf_op jit(solution)/shard_map/ppermute | solution.py:324
  23.7 14.2 %collective-permute-start.7 = (bf16[256,256]{1,0:T(8,128)(2,1)S(1)}, bf16[256,256]{1,0:T(8,128)(2,1)S(1)}, u32[]{:S(2)}, u32[]{:S(2)}) collective-permute-start(bf16[256,256]{1,0:T(8,128)(2,1)S(1)} %get-tuple-element.124.refs_1_.refs_2_), channel_id=1, source_target_pairs={{0,8},{32,40},{48,56},{64,72},{96,104},{112,120},{128,136},{160,16... | collective-permute-start | bytes 393224 | tf_op jit(solution)/shard_map/ppermute | solution.py:330
  25.0 13.4 %collective-permute-start.11 = (bf16[256,256]{1,0:T(8,128)(2,1)S(1)}, bf16[256,256]{1,0:T(8,128)(2,1)S(1)}, u32[]{:S(2)}, u32[]{:S(2)}) collective-permute-start(bf16[256,256]{1,0:T(8,128)(2,1)S(1)} %get-tuple-element.101.refs_5_), channel_id=1, source_target_pairs={{56,64},{120,128},{184,192},{248,256},{312,320},{376,384},{440,448... | collective-permute-start | bytes 393224 | tf_op jit(solution)/shard_map/ppermute | solution.py:326
  25.7 12.8 %collective-permute-start.10 = (bf16[256,256]{1,0:T(8,128)(2,1)S(1)}, bf16[256,256]{1,0:T(8,128)(2,1)S(1)}, u32[]{:S(2)}, u32[]{:S(2)}) collective-permute-start(bf16[256,256]{1,0:T(8,128)(2,1)S(1)} %get-tuple-element.121.refs_6_), channel_id=1, source_target_pairs={{24,32},{40,48},{88,96},{104,112},{152,160},{168,176},{216,224},{2... | collective-permute-start | bytes 393224 | tf_op jit(solution)/shard_map/ppermute | solution.py:324
  38.6 16.2 %collective-permute-start.12 = (bf16[256,256]{1,0:T(8,128)(2,1)S(1)}, bf16[256,256]{1,0:T(8,128)(2,1)S(1)}, u32[]{:S(2)}, u32[]{:S(2)}) collective-permute-start(bf16[256,256]{1,0:T(8,128)(2,1)S(1)} %get-tuple-element.134.refs_1_.refs_2_), channel_id=1, source_target_pairs={{0,8},{32,40},{48,56},{64,72},{96,104},{112,120},{128,136},{160,16... | collective-permute-start | bytes 393224 | tf_op jit(solution)/shard_map/ppermute | solution.py:330
  39.9 15.4 %collective-permute-start.9 = (bf16[256,256]{1,0:T(8,128)(2,1)S(1)}, bf16[256,256]{1,0:T(8,128)(2,1)S(1)}, u32[]{:S(2)}, u32[]{:S(2)}) collective-permute-start(bf16[256,256]{1,0:T(8,128)(2,1)S(1)} %get-tuple-element.111.refs_5_), channel_id=1, source_target_pairs={{56,64},{120,128},{184,192},{248,256},{312,320},{376,384},{440,448... | collective-permute-start | bytes 393224 | tf_op jit(solution)/shard_map/ppermute | solution.py:326
  40.5 14.8 %collective-permute-start.8 = (bf16[256,256]{1,0:T(8,128)(2,1)S(1)}, bf16[256,256]{1,0:T(8,128)(2,1)S(1)}, u32[]{:S(2)}, u32[]{:S(2)}) collective-permute-start(bf16[256,256]{1,0:T(8,128)(2,1)S(1)} %get-tuple-element.131.refs_6_), channel_id=1, source_target_pairs={{8,16},{40,48},{72,80},{104,112},{136,144},{168,176},{200,208},{23... | collective-permute-start | bytes 393224 | tf_op jit(solution)/shard_map/ppermute | solution.py:324
  55.4 16.2 %collective-permute-start.13 = (bf16[256,256]{1,0:T(8,128)(2,1)S(1)}, bf16[256,256]{1,0:T(8,128)(2,1)S(1)}, u32[]{:S(2)}, u32[]{:S(2)}) collective-permute-start(bf16[256,256]{1,0:T(8,128)(2,1)S(1)} %get-tuple-element.144.refs_1_.refs_2_), channel_id=1, source_target_pairs={{0,8},{16,24},{48,56},{64,72},{80,88},{112,120},{128,136},{144,152... | collective-permute-start | bytes 393224 | tf_op jit(solution)/shard_map/ppermute | solution.py:330
  56.7 15.4 %collective-permute-start.17 = (bf16[256,256]{1,0:T(8,128)(2,1)S(1)}, bf16[256,256]{1,0:T(8,128)(2,1)S(1)}, u32[]{:S(2)}, u32[]{:S(2)}) collective-permute-start(bf16[256,256]{1,0:T(8,128)(2,1)S(1)} %get-tuple-element.121.refs_6_), channel_id=1, source_target_pairs={{56,64},{120,128},{184,192},{248,256},{312,320},{376,384},{440,448... | collective-permute-start | bytes 393224 | tf_op jit(solution)/shard_map/ppermute | solution.py:326
  57.4 14.8 %collective-permute-start.16 = (bf16[256,256]{1,0:T(8,128)(2,1)S(1)}, bf16[256,256]{1,0:T(8,128)(2,1)S(1)}, u32[]{:S(2)}, u32[]{:S(2)}) collective-permute-start(bf16[256,256]{1,0:T(8,128)(2,1)S(1)} %get-tuple-element.141.refs_6_), channel_id=1, source_target_pairs={{8,16},{40,48},{72,80},{104,112},{136,144},{168,176},{200,208},{23... | collective-permute-start | bytes 393224 | tf_op jit(solution)/shard_map/ppermute | solution.py:324
  72.2 16.2 %collective-permute-start.18 = (bf16[256,256]{1,0:T(8,128)(2,1)S(1)}, bf16[256,256]{1,0:T(8,128)(2,1)S(1)}, u32[]{:S(2)}, u32[]{:S(2)}) collective-permute-start(bf16[256,256]{1,0:T(8,128)(2,1)S(1)} %get-tuple-element.154.refs_1_.refs_2_), channel_id=1, source_target_pairs={{0,8},{16,24},{48,56},{64,72},{80,88},{112,120},{128,136},{144,152... | collective-permute-start | bytes 393224 | tf_op jit(solution)/shard_map/ppermute | solution.py:330
  73.5 15.4 %collective-permute-start.15 = (bf16[256,256]{1,0:T(8,128)(2,1)S(1)}, bf16[256,256]{1,0:T(8,128)(2,1)S(1)}, u32[]{:S(2)}, u32[]{:S(2)}) collective-permute-start(bf16[256,256]{1,0:T(8,128)(2,1)S(1)} %get-tuple-element.131.refs_6_), channel_id=1, source_target_pairs={{56,64},{120,128},{184,192},{248,256},{312,320},{376,384},{440,448... | collective-permute-start | bytes 393224 | tf_op jit(solution)/shard_map/ppermute | solution.py:326
  74.2 14.8 %collective-permute-start.14 = (bf16[256,256]{1,0:T(8,128)(2,1)S(1)}, bf16[256,256]{1,0:T(8,128)(2,1)S(1)}, u32[]{:S(2)}, u32[]{:S(2)}) collective-permute-start(bf16[256,256]{1,0:T(8,128)(2,1)S(1)} %get-tuple-element.151.refs_6_), channel_id=1, source_target_pairs={{8,16},{24,32},{72,80},{88,96},{136,144},{152,160},{200,208},{216,... | collective-permute-start | bytes 393224 | tf_op jit(solution)/shard_map/ppermute | solution.py:324
  89.1 16.2 %collective-permute-start.19 = (bf16[256,256]{1,0:T(8,128)(2,1)S(1)}, bf16[256,256]{1,0:T(8,128)(2,1)S(1)}, u32[]{:S(2)}, u32[]{:S(2)}) collective-permute-start(bf16[256,256]{1,0:T(8,128)(2,1)S(1)} %get-tuple-element.164.refs_1_.refs_2_), channel_id=1, source_target_pairs={{0,8},{16,24},{32,40},{64,72},{80,88},{96,104},{128,136},{144,152}... | collective-permute-start | bytes 393224 | tf_op jit(solution)/shard_map/ppermute | solution.py:330
  90.4 15.4 %collective-permute-start.23 = (bf16[256,256]{1,0:T(8,128)(2,1)S(1)}, bf16[256,256]{1,0:T(8,128)(2,1)S(1)}, u32[]{:S(2)}, u32[]{:S(2)}) collective-permute-start(bf16[256,256]{1,0:T(8,128)(2,1)S(1)} %get-tuple-element.141.refs_6_), channel_id=1, source_target_pairs={{56,64},{120,128},{184,192},{248,256},{312,320},{376,384},{440,448... | collective-permute-start | bytes 393224 | tf_op jit(solution)/shard_map/ppermute | solution.py:326
  91.0 14.8 %collective-permute-start.22 = (bf16[256,256]{1,0:T(8,128)(2,1)S(1)}, bf16[256,256]{1,0:T(8,128)(2,1)S(1)}, u32[]{:S(2)}, u32[]{:S(2)}) collective-permute-start(bf16[256,256]{1,0:T(8,128)(2,1)S(1)} %get-tuple-element.161.refs_6_), channel_id=1, source_target_pairs={{8,16},{24,32},{72,80},{88,96},{136,144},{152,160},{200,208},{216,... | collective-permute-start | bytes 393224 | tf_op jit(solution)/shard_map/ppermute | solution.py:324
  105.9 16.2 %collective-permute-start.24 = (bf16[256,256]{1,0:T(8,128)(2,1)S(1)}, bf16[256,256]{1,0:T(8,128)(2,1)S(1)}, u32[]{:S(2)}, u32[]{:S(2)}) collective-permute-start(bf16[256,256]{1,0:T(8,128)(2,1)S(1)} %get-tuple-element.174.refs_1_.refs_2_), channel_id=1, source_target_pairs={{0,8},{16,24},{32,40},{64,72},{80,88},{96,104},{128,136},{144,152}... | collective-permute-start | bytes 393224 | tf_op jit(solution)/shard_map/ppermute | solution.py:330
  107.2 15.4 %collective-permute-start.21 = (bf16[256,256]{1,0:T(8,128)(2,1)S(1)}, bf16[256,256]{1,0:T(8,128)(2,1)S(1)}, u32[]{:S(2)}, u32[]{:S(2)}) collective-permute-start(bf16[256,256]{1,0:T(8,128)(2,1)S(1)} %get-tuple-element.151.refs_6_), channel_id=1, source_target_pairs={{56,64},{120,128},{184,192},{248,256},{312,320},{376,384},{440,448... | collective-permute-start | bytes 393224 | tf_op jit(solution)/shard_map/ppermute | solution.py:326
  107.9 14.8 %collective-permute-start.20 = (bf16[256,256]{1,0:T(8,128)(2,1)S(1)}, bf16[256,256]{1,0:T(8,128)(2,1)S(1)}, u32[]{:S(2)}, u32[]{:S(2)}) collective-permute-start(bf16[256,256]{1,0:T(8,128)(2,1)S(1)} %get-tuple-element.171.refs_6_), channel_id=1, source_target_pairs={{8,16},{24,32},{40,48},{72,80},{88,96},{104,112},{136,144},{152,16... | collective-permute-start | bytes 393224 | tf_op jit(solution)/shard_map/ppermute | solution.py:324
  122.7 9.1 %collective-permute-start.25 = (bf16[64,8,128]{2,1,0:T(8,128)(2,1)S(1)}, bf16[64,8,128]{2,1,0:T(8,128)(2,1)}, u32[]{:S(2)}, u32[]{:S(2)}) collective-permute-start(bf16[64,8,128]{2,1,0:T(8,128)(2,1)S(1)} %bitcast.46), channel_id=1, source_target_pairs={{0,1},{1,2},{2,3},{3,452},{4,5},{5,6},{6,7},{7,448},{8,9},{9,10},{... | collective-permute-start | bytes 393224 | tf_op jit(solution)/shard_map/ppermute | solution.py:363
  131.9 39.1 %all-to-all-start = ((bf16[64,8,128]{2,1,0:T(8,128)(2,1)}), bf16[64,8,128]{2,1,0:T(8,128)(2,1)S(1)}, u32[]{:S(2)}, u32[]{:S(2)}) async-start(bf16[64,8,128]{2,1,0:T(8,128)(2,1)} %collective-permute-done.25), calls=%async_computation | async-start | bytes 262144 | tf_op jit(solution)/shard_map/all_to_all | solution.py:364
  172.6 35.9 %all-to-all-start.1 = ((bf16[64,4,8,128]{3,2,1,0:T(8,128)(2,1)}), bf16[64,4,8,128]{3,2,1,0:T(8,128)(2,1)S(1)}, u32[]{:S(2)}, u32[]{:S(2)}) async-start(bf16[64,4,8,128]{3,2,1,0:T(8,128)(2,1)} %shard_map.107), calls=%async_computation.1 | async-start | bytes 1048576 | tf_op jit(solution)/shard_map/all_to_all | solution.py:372
  (12 other events, 106.6 us)

commit v4 on v3

--- a/solution.py
+++ b/solution.py
@@ -65,9 +65,9 @@
     return active, stop, jnp.logical_and(late, inner == 0), lax.rem(inner, 2)
 
 
-def fetch(stop, count, row_ref, user_ref, low_ref, rated_ref, tiles, copy):
-    tile = tiles.shape[1]
-    for c in range(tiles.shape[0]):
+def fetch(stop, count, row_ref, user_ref, low_ref, rated_ref, tiles, copy=None):
+    tile = tiles.shape[-1]
+    for c in range(tiles.shape[-3]):
         rows = pl.ds(c * tile, tile)
 
         @pl.when(c < count)
@@ -80,13 +80,14 @@
             low_ref[rows, :] = jnp.zeros((tile, low_ref.shape[1]), BF16)
             rated_ref[:, rows] = jnp.zeros((rated_ref.shape[0], tile), BF16)
 
-    copy.wait()
-    for c in range(tiles.shape[0]):
+    if copy is not None:
+        copy.wait()
+    for c in range(tiles.shape[-3]):
         rows = pl.ds(c * tile, tile)
 
         @pl.when(c < count)
         def _():
-            rated_ref[:, rows] = tiles[c].T
+            rated_ref[:, rows] = (tiles[c] if copy is not None else tiles[stop, c]).T
 
 
 def update_items(exact, item_low, decay, low_ref, rated_ref, residual_ref, item_ref):
@@ -179,14 +180,13 @@
     if last:
         (out_ref,) = refs
     else:
-        ratings_ref, out_ref, low_ref, rated_ref, decay_ref, tiles, sem = refs
+        ratings_ref, out_ref, low_ref, rated_ref, decay_ref = refs
         next_active, next_stop, _, _ = plan_slot(slot + 1, stops)
         next_count = jnp.where(next_active, count_ref[next_stop], 0)
         decay_ref[...] = jnp.full(decay_ref.shape, shrinkage * next_count.astype(F32))
-        copy = pltpu.make_async_copy(ratings_ref.at[next_stop], tiles, sem)
-        pl.when(next_active)(copy.start)
     tile = item_ref.shape[0]
-    out_ref[...] = user_ref[...]
+    if last or slot == 0:
+        out_ref[...] = user_ref[...]
     for c in range(residual_ref.shape[1] // tile):
 
         @pl.when(c < count)
@@ -205,7 +205,7 @@
 
         @pl.when(next_active)
         def _():
-            fetch(next_stop, next_count, row_ref, out_ref, low_ref, rated_ref, tiles, copy)
+            fetch(next_stop, next_count, row_ref, out_ref, low_ref, rated_ref, ratings_ref)
 
 
 def route_body(stops, plan_ref, index_ref, filled):
@@ -339,9 +339,9 @@
             users, low, rated, decay = call(
                 body,
                 (user_shape, low_shape, rated_shape, decay_shape),
-                [SMEM, SMEM, VMEM, VMEM, VMEM, ANY],
+                [SMEM, SMEM, VMEM, VMEM, VMEM, VMEM],
                 (VMEM, VMEM, VMEM, VMEM),
-                tile_scratch,
+                (),
                 flops,
                 alias={4: 0} if slot else {},
             )(*operands, rating_tiles)

time: 210 us -> 210 us (level)
  transfers between devices with their start and end apart: 28 -> 28, of which waited for: 10 -> 10; matrix products, arithmetic and copies ran while one was open for 0% -> 0% of each run, Pallas kernels for 9% -> 8%
where the time goes in v4:
time: 210 us; the launch traced here: 209 us
  waiting for transfers between devices  117 us (56%)
  starting transfers between devices  65.6 us (31%)
  Pallas kernels  23.3 us (11%)
    ppermute x9, waiting for transfers between devices, shards(): from_even = lax.ppermute(block, 'blk', within(slot, 0))  69.7 us
    all_to_all x1, waiting for transfers between devices, shards(): lax.all_to_all(picked, 'blk', split_axis=0, concat_axis=0, tiled=True)  28.3 us
    all_to_all x1, starting transfers between devices, shards(): lax.all_to_all(shifted, 'blk', split_axis=0, concat_axis=0, tiled=True)  24.3 us
    ppermute x9, starting transfers between devices, shards(): from_odd = lax.ppermute(odd_block, 'blk', within(slot, 1))  17.2 us
    all_to_all x1, waiting for transfers between devices, shards(): lax.all_to_all(shifted, 'blk', split_axis=0, concat_axis=0, tiled=True)  12.1 us
    ppermute x9, starting transfers between devices, shards(): from_even = lax.ppermute(block, 'blk', within(slot, 0))  10.5 us
    pallas_call x9, Pallas kernels, shards(): call(body, (user_shape, low_shape, rated_shape, decay_shape), [SMEM, SMEM...  9.29 us
    ppermute x1, waiting for transfers between devices, shards(): shifted = lax.ppermute(pieces, ('blk', 'group'), moves)  5.92 us
  transfers between devices with their start and end apart: 28, of which 10 were waited for; matrix products, arithmetic and copies ran while one was open for 0% of the time, Pallas kernels for 8%

profile of v4, /device:TPU:1, one launch (start us, length us, event | category | flops | bytes accessed | tf_op | source)
XLA Modules:
  0.0 209.2 jit_solution(2638678667084011874)
XLA Ops:
  0.7 2.9 %shard_map.77 = (bf16[256,256]{1,0:T(8,128)(2,1)}, bf16[256,512]{1,0:T(8,128)(2,1)}, bf16[256,256]{1,0:T(8,128)(2,1)}) custom-call(s32[8]{0:T(128)} %bitcast.35, s32[2,8]{1,0:T(2,128)} %bitcast.24, f32[1024,256]{1,0:T(8,128)} %bitcast.21, f32[256,256]{1,0:T(8,128)} %bitcast.49, bf16[8,2,256,256]{3,2,1,0:T(8,128)(2,1)} %bitcast.11), custom_call_target="tpu_custom_call" | custom-call | flops 134217728 | bytes 1048576 | tf_op jit(solution)/shard_map/pallas_call | solution.py:271
  3.6 1.4 collective-permute-start.1
  5.0 4.8 %collective-permute-start = (bf16[256,256]{1,0:T(8,128)(2,1)}, bf16[256,256]{1,0:T(8,128)(2,1)S(1)}, u32[]{:S(2)}, u32[]{:S(2)}) collective-permute-start(bf16[256,256]{1,0:T(8,128)(2,1)} %get-tuple-element.95.refs_1_), channel_id=1, source_target_pairs={{8,16},{24,32},{40,48},{72,80},{88,96},{104,112},{136,144},{152,16... | collective-permute-start | bytes 393224 | tf_op jit(solution)/shard_map/ppermute | solution.py:324
  14.2 4.6 %collective-permute-start.5 = (bf16[256,256]{1,0:T(8,128)(2,1)S(1)}, bf16[256,256]{1,0:T(8,128)(2,1)S(1)}, u32[]{:S(2)}, u32[]{:S(2)}) collective-permute-start(bf16[256,256]{1,0:T(8,128)(2,1)S(1)} %get-tuple-element.101.refs_5_), channel_id=1, source_target_pairs={{8,16},{24,32},{40,48},{72,80},{88,96},{104,112},{136,144},{152,16... | collective-permute-start | bytes 393224 | tf_op jit(solution)/shard_map/ppermute | solution.py:324
  27.0 10.9 %collective-permute-done.7.refs_0_ = bf16[256,256]{1,0:T(8,128)(2,1)S(1)} collective-permute-done((bf16[256,256]{1,0:T(8,128)(2,1)S(1)}, bf16[256,256]{1,0:T(8,128)(2,1)S(1)}, u32[]{:S(2)}, u32[]{:S(2)}) %collective-permute-start.7) | collective-permute-done | bytes 131104 | tf_op jit(solution)/shard_map/ppermute | solution.py:330
  40.5 1.3 collective-permute-start.8
  43.1 11.7 %collective-permute-done.12.refs_0_ = bf16[256,256]{1,0:T(8,128)(2,1)S(1)} collective-permute-done((bf16[256,256]{1,0:T(8,128)(2,1)S(1)}, bf16[256,256]{1,0:T(8,128)(2,1)S(1)}, u32[]{:S(2)}, u32[]{:S(2)}) %collective-permute-start.12) | collective-permute-done | bytes 131104 | tf_op jit(solution)/shard_map/ppermute | solution.py:330
  57.4 1.3 collective-permute-start.16
  59.9 11.7 %collective-permute-done.13.refs_0_ = bf16[256,256]{1,0:T(8,128)(2,1)S(1)} collective-permute-done((bf16[256,256]{1,0:T(8,128)(2,1)S(1)}, bf16[256,256]{1,0:T(8,128)(2,1)S(1)}, u32[]{:S(2)}, u32[]{:S(2)}) %collective-permute-start.13) | collective-permute-done | bytes 131104 | tf_op jit(solution)/shard_map/ppermute | solution.py:330
  74.2 1.3 collective-permute-start.14
  76.8 11.7 %collective-permute-done.18.refs_0_ = bf16[256,256]{1,0:T(8,128)(2,1)S(1)} collective-permute-done((bf16[256,256]{1,0:T(8,128)(2,1)S(1)}, bf16[256,256]{1,0:T(8,128)(2,1)S(1)}, u32[]{:S(2)}, u32[]{:S(2)}) %collective-permute-start.18) | collective-permute-done | bytes 131104 | tf_op jit(solution)/shard_map/ppermute | solution.py:330
  91.0 1.3 collective-permute-start.22
  93.5 11.8 %collective-permute-done.19.refs_0_ = bf16[256,256]{1,0:T(8,128)(2,1)S(1)} collective-permute-done((bf16[256,256]{1,0:T(8,128)(2,1)S(1)}, bf16[256,256]{1,0:T(8,128)(2,1)S(1)}, u32[]{:S(2)}, u32[]{:S(2)}) %collective-permute-start.19) | collective-permute-done | bytes 131104 | tf_op jit(solution)/shard_map/ppermute | solution.py:330
  107.9 1.3 collective-permute-start.20
  110.1 12.0 %collective-permute-done.24.refs_0_ = bf16[256,256]{1,0:T(8,128)(2,1)S(1)} collective-permute-done((bf16[256,256]{1,0:T(8,128)(2,1)S(1)}, bf16[256,256]{1,0:T(8,128)(2,1)S(1)}, u32[]{:S(2)}, u32[]{:S(2)}) %collective-permute-start.24) | collective-permute-done | bytes 131104 | tf_op jit(solution)/shard_map/ppermute | solution.py:330
  122.7 3.2 %collective-permute-start.25 = (bf16[64,8,128]{2,1,0:T(8,128)(2,1)S(1)}, bf16[64,8,128]{2,1,0:T(8,128)(2,1)}, u32[]{:S(2)}, u32[]{:S(2)}) collective-permute-start(bf16[64,8,128]{2,1,0:T(8,128)(2,1)S(1)} %bitcast.46), channel_id=1, source_target_pairs={{0,1},{1,2},{2,3},{3,452},{4,5},{5,6},{6,7},{7,448},{8,9},{9,10},{... | collective-permute-start | bytes 393224 | tf_op jit(solution)/shard_map/ppermute | solution.py:363
  126.0 5.9 %collective-permute-done.25 = bf16[64,8,128]{2,1,0:T(8,128)(2,1)} collective-permute-done((bf16[64,8,128]{2,1,0:T(8,128)(2,1)S(1)}, bf16[64,8,128]{2,1,0:T(8,128)(2,1)}, u32[]{:S(2)}, u32[]{:S(2)}) %collective-permute-start.25) | collective-permute-done | bytes 131104 | tf_op jit(solution)/shard_map/ppermute | solution.py:363
  131.9 24.3 %all-to-all-start = ((bf16[64,8,128]{2,1,0:T(8,128)(2,1)}), bf16[64,8,128]{2,1,0:T(8,128)(2,1)S(1)}, u32[]{:S(2)}, u32[]{:S(2)}) async-start(bf16[64,8,128]{2,1,0:T(8,128)(2,1)} %collective-permute-done.25), calls=%async_computation | async-start | bytes 262144 | tf_op jit(solution)/shard_map/all_to_all | solution.py:364
  156.2 2.5 %shard_map.106.index_ref = s32[256]{0:T(256)S(1)} custom-call(s32[8,64]{1,0:T(8,128)S(1)} %copy-done.7), custom_call_target="tpu_custom_call" | custom-call | bytes 256 | tf_op jit(solution)/shard_map/pallas_call | solution.py:350
  158.7 12.1 %all-to-all-done.pieces_ref = bf16[64,8,128]{2,1,0:T(8,128)(2,1)S(1)} async-done(((bf16[64,8,128]{2,1,0:T(8,128)(2,1)}), bf16[64,8,128]{2,1,0:T(8,128)(2,1)S(1)}, u32[]{:S(2)}, u32[]{:S(2)}) %all-to-all-start) | async-done | bytes 131104 | tf_op jit(solution)/shard_map/all_to_all | solution.py:364
  170.8 1.6 shard_map.107
  172.4 5.8 %all-to-all-start.1 = ((bf16[64,4,8,128]{3,2,1,0:T(8,128)(2,1)}), bf16[64,4,8,128]{3,2,1,0:T(8,128)(2,1)S(1)}, u32[]{:S(2)}, u32[]{:S(2)}) async-start(bf16[64,4,8,128]{3,2,1,0:T(8,128)(2,1)} %shard_map.107), calls=%async_computation.1 | async-start | bytes 1048576 | tf_op jit(solution)/shard_map/all_to_all | solution.py:372
  178.2 1.8 shard_map.105
  180.0 28.3 %all-to-all-done.1 = bf16[64,4,8,128]{3,2,1,0:T(8,128)(2,1)S(1)} async-done(((bf16[64,4,8,128]{3,2,1,0:T(8,128)(2,1)}), bf16[64,4,8,128]{3,2,1,0:T(8,128)(2,1)S(1)}, u32[]{:S(2)}, u32[]{:S(2)}) %all-to-all-start.1) | async-done | bytes 524320 | tf_op jit(solution)/shard_map/all_to_all | solution.py:372
  (80 shorter events, 32.5 us)
Async XLA Ops:
  3.6 9.3 %collective-permute-start.1 = (bf16[256,256]{1,0:T(8,128)(2,1)}, bf16[256,256]{1,0:T(8,128)(2,1)S(1)}, u32[]{:S(2)}, u32[]{:S(2)}) collective-permute-start(bf16[256,256]{1,0:T(8,128)(2,1)} %get-tuple-element.95.refs_1_), channel_id=1, source_target_pairs={{0,8},{16,24},{32,40},{48,56},{64,72},{80,88},{96,104},{112,120},{... | collective-permute-start | bytes 393224 | tf_op jit(solution)/shard_map/ppermute | solution.py:330
  5.0 8.5 %collective-permute-start = (bf16[256,256]{1,0:T(8,128)(2,1)}, bf16[256,256]{1,0:T(8,128)(2,1)S(1)}, u32[]{:S(2)}, u32[]{:S(2)}) collective-permute-start(bf16[256,256]{1,0:T(8,128)(2,1)} %get-tuple-element.95.refs_1_), channel_id=1, source_target_pairs={{8,16},{24,32},{40,48},{72,80},{88,96},{104,112},{136,144},{152,16... | collective-permute-start | bytes 393224 | tf_op jit(solution)/shard_map/ppermute | solution.py:324
  14.2 6.5 %collective-permute-start.5 = (bf16[256,256]{1,0:T(8,128)(2,1)S(1)}, bf16[256,256]{1,0:T(8,128)(2,1)S(1)}, u32[]{:S(2)}, u32[]{:S(2)}) collective-permute-start(bf16[256,256]{1,0:T(8,128)(2,1)S(1)} %get-tuple-element.101.refs_5_), channel_id=1, source_target_pairs={{8,16},{24,32},{40,48},{72,80},{88,96},{104,112},{136,144},{152,16... | collective-permute-start | bytes 393224 | tf_op jit(solution)/shard_map/ppermute | solution.py:324
  23.5 14.4 %collective-permute-start.7 = (bf16[256,256]{1,0:T(8,128)(2,1)S(1)}, bf16[256,256]{1,0:T(8,128)(2,1)S(1)}, u32[]{:S(2)}, u32[]{:S(2)}) collective-permute-start(bf16[256,256]{1,0:T(8,128)(2,1)S(1)} %get-tuple-element.124.refs_1_.refs_2_), channel_id=1, source_target_pairs={{0,8},{32,40},{48,56},{64,72},{96,104},{112,120},{128,136},{160,16... | collective-permute-start | bytes 393224 | tf_op jit(solution)/shard_map/ppermute | solution.py:330
  24.8 13.6 %collective-permute-start.11 = (bf16[256,256]{1,0:T(8,128)(2,1)S(1)}, bf16[256,256]{1,0:T(8,128)(2,1)S(1)}, u32[]{:S(2)}, u32[]{:S(2)}) collective-permute-start(bf16[256,256]{1,0:T(8,128)(2,1)S(1)} %get-tuple-element.101.refs_5_), channel_id=1, source_target_pairs={{56,64},{120,128},{184,192},{248,256},{312,320},{376,384},{440,448... | collective-permute-start | bytes 393224 | tf_op jit(solution)/shard_map/ppermute | solution.py:326
  25.5 13.0 %collective-permute-start.10 = (bf16[256,256]{1,0:T(8,128)(2,1)S(1)}, bf16[256,256]{1,0:T(8,128)(2,1)S(1)}, u32[]{:S(2)}, u32[]{:S(2)}) collective-permute-start(bf16[256,256]{1,0:T(8,128)(2,1)S(1)} %get-tuple-element.121.refs_6_), channel_id=1, source_target_pairs={{24,32},{40,48},{88,96},{104,112},{152,160},{168,176},{216,224},{2... | collective-permute-start | bytes 393224 | tf_op jit(solution)/shard_map/ppermute | solution.py:324
  38.6 16.2 %collective-permute-start.12 = (bf16[256,256]{1,0:T(8,128)(2,1)S(1)}, bf16[256,256]{1,0:T(8,128)(2,1)S(1)}, u32[]{:S(2)}, u32[]{:S(2)}) collective-permute-start(bf16[256,256]{1,0:T(8,128)(2,1)S(1)} %get-tuple-element.134.refs_1_.refs_2_), channel_id=1, source_target_pairs={{0,8},{32,40},{48,56},{64,72},{96,104},{112,120},{128,136},{160,16... | collective-permute-start | bytes 393224 | tf_op jit(solution)/shard_map/ppermute | solution.py:330
  39.9 15.4 %collective-permute-start.9 = (bf16[256,256]{1,0:T(8,128)(2,1)S(1)}, bf16[256,256]{1,0:T(8,128)(2,1)S(1)}, u32[]{:S(2)}, u32[]{:S(2)}) collective-permute-start(bf16[256,256]{1,0:T(8,128)(2,1)S(1)} %get-tuple-element.111.refs_5_), channel_id=1, source_target_pairs={{56,64},{120,128},{184,192},{248,256},{312,320},{376,384},{440,448... | collective-permute-start | bytes 393224 | tf_op jit(solution)/shard_map/ppermute | solution.py:326
  40.5 14.8 %collective-permute-start.8 = (bf16[256,256]{1,0:T(8,128)(2,1)S(1)}, bf16[256,256]{1,0:T(8,128)(2,1)S(1)}, u32[]{:S(2)}, u32[]{:S(2)}) collective-permute-start(bf16[256,256]{1,0:T(8,128)(2,1)S(1)} %get-tuple-element.131.refs_6_), channel_id=1, source_target_pairs={{8,16},{40,48},{72,80},{104,112},{136,144},{168,176},{200,208},{23... | collective-permute-start | bytes 393224 | tf_op jit(solution)/shard_map/ppermute | solution.py:324
  55.4 16.2 %collective-permute-start.13 = (bf16[256,256]{1,0:T(8,128)(2,1)S(1)}, bf16[256,256]{1,0:T(8,128)(2,1)S(1)}, u32[]{:S(2)}, u32[]{:S(2)}) collective-permute-start(bf16[256,256]{1,0:T(8,128)(2,1)S(1)} %get-tuple-element.144.refs_1_.refs_2_), channel_id=1, source_target_pairs={{0,8},{16,24},{48,56},{64,72},{80,88},{112,120},{128,136},{144,152... | collective-permute-start | bytes 393224 | tf_op jit(solution)/shard_map/ppermute | solution.py:330
  56.7 15.4 %collective-permute-start.17 = (bf16[256,256]{1,0:T(8,128)(2,1)S(1)}, bf16[256,256]{1,0:T(8,128)(2,1)S(1)}, u32[]{:S(2)}, u32[]{:S(2)}) collective-permute-start(bf16[256,256]{1,0:T(8,128)(2,1)S(1)} %get-tuple-element.121.refs_6_), channel_id=1, source_target_pairs={{56,64},{120,128},{184,192},{248,256},{312,320},{376,384},{440,448... | collective-permute-start | bytes 393224 | tf_op jit(solution)/shard_map/ppermute | solution.py:326
  57.4 14.8 %collective-permute-start.16 = (bf16[256,256]{1,0:T(8,128)(2,1)S(1)}, bf16[256,256]{1,0:T(8,128)(2,1)S(1)}, u32[]{:S(2)}, u32[]{:S(2)}) collective-permute-start(bf16[256,256]{1,0:T(8,128)(2,1)S(1)} %get-tuple-element.141.refs_6_), channel_id=1, source_target_pairs={{8,16},{40,48},{72,80},{104,112},{136,144},{168,176},{200,208},{23... | collective-permute-start | bytes 393224 | tf_op jit(solution)/shard_map/ppermute | solution.py:324
  72.2 16.2 %collective-permute-start.18 = (bf16[256,256]{1,0:T(8,128)(2,1)S(1)}, bf16[256,256]{1,0:T(8,128)(2,1)S(1)}, u32[]{:S(2)}, u32[]{:S(2)}) collective-permute-start(bf16[256,256]{1,0:T(8,128)(2,1)S(1)} %get-tuple-element.154.refs_1_.refs_2_), channel_id=1, source_target_pairs={{0,8},{16,24},{48,56},{64,72},{80,88},{112,120},{128,136},{144,152... | collective-permute-start | bytes 393224 | tf_op jit(solution)/shard_map/ppermute | solution.py:330
  73.5 15.4 %collective-permute-start.15 = (bf16[256,256]{1,0:T(8,128)(2,1)S(1)}, bf16[256,256]{1,0:T(8,128)(2,1)S(1)}, u32[]{:S(2)}, u32[]{:S(2)}) collective-permute-start(bf16[256,256]{1,0:T(8,128)(2,1)S(1)} %get-tuple-element.131.refs_6_), channel_id=1, source_target_pairs={{56,64},{120,128},{184,192},{248,256},{312,320},{376,384},{440,448... | collective-permute-start | bytes 393224 | tf_op jit(solution)/shard_map/ppermute | solution.py:326
  74.2 14.8 %collective-permute-start.14 = (bf16[256,256]{1,0:T(8,128)(2,1)S(1)}, bf16[256,256]{1,0:T(8,128)(2,1)S(1)}, u32[]{:S(2)}, u32[]{:S(2)}) collective-permute-start(bf16[256,256]{1,0:T(8,128)(2,1)S(1)} %get-tuple-element.151.refs_6_), channel_id=1, source_target_pairs={{8,16},{24,32},{72,80},{88,96},{136,144},{152,160},{200,208},{216,... | collective-permute-start | bytes 393224 | tf_op jit(solution)/shard_map/ppermute | solution.py:324
  89.1 16.2 %collective-permute-start.19 = (bf16[256,256]{1,0:T(8,128)(2,1)S(1)}, bf16[256,256]{1,0:T(8,128)(2,1)S(1)}, u32[]{:S(2)}, u32[]{:S(2)}) collective-permute-start(bf16[256,256]{1,0:T(8,128)(2,1)S(1)} %get-tuple-element.164.refs_1_.refs_2_), channel_id=1, source_target_pairs={{0,8},{16,24},{32,40},{64,72},{80,88},{96,104},{128,136},{144,152}... | collective-permute-start | bytes 393224 | tf_op jit(solution)/shard_map/ppermute | solution.py:330
  90.4 15.4 %collective-permute-start.23 = (bf16[256,256]{1,0:T(8,128)(2,1)S(1)}, bf16[256,256]{1,0:T(8,128)(2,1)S(1)}, u32[]{:S(2)}, u32[]{:S(2)}) collective-permute-start(bf16[256,256]{1,0:T(8,128)(2,1)S(1)} %get-tuple-element.141.refs_6_), channel_id=1, source_target_pairs={{56,64},{120,128},{184,192},{248,256},{312,320},{376,384},{440,448... | collective-permute-start | bytes 393224 | tf_op jit(solution)/shard_map/ppermute | solution.py:326
  91.0 14.8 %collective-permute-start.22 = (bf16[256,256]{1,0:T(8,128)(2,1)S(1)}, bf16[256,256]{1,0:T(8,128)(2,1)S(1)}, u32[]{:S(2)}, u32[]{:S(2)}) collective-permute-start(bf16[256,256]{1,0:T(8,128)(2,1)S(1)} %get-tuple-element.161.refs_6_), channel_id=1, source_target_pairs={{8,16},{24,32},{72,80},{88,96},{136,144},{152,160},{200,208},{216,... | collective-permute-start | bytes 393224 | tf_op jit(solution)/shard_map/ppermute | solution.py:324
  105.9 16.2 %collective-permute-start.24 = (bf16[256,256]{1,0:T(8,128)(2,1)S(1)}, bf16[256,256]{1,0:T(8,128)(2,1)S(1)}, u32[]{:S(2)}, u32[]{:S(2)}) collective-permute-start(bf16[256,256]{1,0:T(8,128)(2,1)S(1)} %get-tuple-element.174.refs_1_.refs_2_), channel_id=1, source_target_pairs={{0,8},{16,24},{32,40},{64,72},{80,88},{96,104},{128,136},{144,152}... | collective-permute-start | bytes 393224 | tf_op jit(solution)/shard_map/ppermute | solution.py:330
  107.2 15.4 %collective-permute-start.21 = (bf16[256,256]{1,0:T(8,128)(2,1)S(1)}, bf16[256,256]{1,0:T(8,128)(2,1)S(1)}, u32[]{:S(2)}, u32[]{:S(2)}) collective-permute-start(bf16[256,256]{1,0:T(8,128)(2,1)S(1)} %get-tuple-element.151.refs_6_), channel_id=1, source_target_pairs={{56,64},{120,128},{184,192},{248,256},{312,320},{376,384},{440,448... | collective-permute-start | bytes 393224 | tf_op jit(solution)/shard_map/ppermute | solution.py:326
  107.9 14.8 %collective-permute-start.20 = (bf16[256,256]{1,0:T(8,128)(2,1)S(1)}, bf16[256,256]{1,0:T(8,128)(2,1)S(1)}, u32[]{:S(2)}, u32[]{:S(2)}) collective-permute-start(bf16[256,256]{1,0:T(8,128)(2,1)S(1)} %get-tuple-element.171.refs_6_), channel_id=1, source_target_pairs={{8,16},{24,32},{40,48},{72,80},{88,96},{104,112},{136,144},{152,16... | collective-permute-start | bytes 393224 | tf_op jit(solution)/shard_map/ppermute | solution.py:324
  122.7 9.1 %collective-permute-start.25 = (bf16[64,8,128]{2,1,0:T(8,128)(2,1)S(1)}, bf16[64,8,128]{2,1,0:T(8,128)(2,1)}, u32[]{:S(2)}, u32[]{:S(2)}) collective-permute-start(bf16[64,8,128]{2,1,0:T(8,128)(2,1)S(1)} %bitcast.46), channel_id=1, source_target_pairs={{0,1},{1,2},{2,3},{3,452},{4,5},{5,6},{6,7},{7,448},{8,9},{9,10},{... | collective-permute-start | bytes 393224 | tf_op jit(solution)/shard_map/ppermute | solution.py:363
  131.9 38.9 %all-to-all-start = ((bf16[64,8,128]{2,1,0:T(8,128)(2,1)}), bf16[64,8,128]{2,1,0:T(8,128)(2,1)S(1)}, u32[]{:S(2)}, u32[]{:S(2)}) async-start(bf16[64,8,128]{2,1,0:T(8,128)(2,1)} %collective-permute-done.25), calls=%async_computation | async-start | bytes 262144 | tf_op jit(solution)/shard_map/all_to_all | solution.py:364
  172.4 35.9 %all-to-all-start.1 = ((bf16[64,4,8,128]{3,2,1,0:T(8,128)(2,1)}), bf16[64,4,8,128]{3,2,1,0:T(8,128)(2,1)S(1)}, u32[]{:S(2)}, u32[]{:S(2)}) async-start(bf16[64,4,8,128]{3,2,1,0:T(8,128)(2,1)} %shard_map.107), calls=%async_computation.1 | async-start | bytes 1048576 | tf_op jit(solution)/shard_map/all_to_all | solution.py:372
  (12 other events, 106.0 us)
